TPU v7x, 32 devices: a whole 2x2x4 slice. The times are simulated.
32 devices in a mesh: wide: 8 (over y, x, core), narrow: 4 (over z).
Axes of the slice: x: 2, y: 2, z: 4, core: 2. Of those that a mesh axis runs over, the one named last changes fastest.
Arguments:
- initial: float32 [2, 256, 128, 128], P(None, 'wide', 'narrow'), may hold values from 0.5 to 2
- images: float32 [2, 4, 24, 24, 128], P(None, None, 'wide', 'narrow'), may hold values from 20 to 200
- blocks: bfloat16 [4, 8, 128, 128], replicated, may hold values from 0 to 0.03125
- lib_index: int32 [4, 256, 128], P(None, 'wide', 'narrow'), may hold values from 0 to 7
- tile_map: int32 [4, 256, 128], P(None, 'wide', 'narrow'), may hold values from 0 to 161
- win_x: int32 [8, 4, 4], P('wide', 'narrow'), may hold values from 0 to 31
- win_y: int32 [8, 4, 4], P('wide', 'narrow'), may hold values from 0 to 31
- win_z: int32 [8, 4, 4], P('wide', 'narrow'), may hold values from 0 to 64
Outputs:
- volume: float32 [2, 256, 128, 128], P(None, 'wide', 'narrow')
- correlation: float32 [8, 4, 4, 4096], P('wide', 'narrow')
All inputs are finite; a program needn't handle non-finite values.
Results may differ from a plain program's by a relative error of at most 0.00062.
Values may be sent and summed in bfloat16 or wider, within the bound.
No kernel may reach another device: no remote copies, remote signals or barrier semaphores. Data moves between devices by JAX's collectives and lax.ppermute only.
A program may use at most 128 MiB of HBM per device.

v0:
```python
import functools
import numpy as np
import jax
import jax.numpy as jnp
from jax import lax
from jax.experimental import pallas as pl
from jax.experimental.pallas import tpu as pltpu
from jax.sharding import PartitionSpec as P

WIN = 64
DISP = 16
SWEEPS = 2
TERMS = 4
LEVELS = 65535.0
MIDDLE = 32768.0
GRAIN = 16.0
SPARE = 16
STEPS = 1
UNROLL = False
LIMIT = 24 * 1024 * 1024
WIDE_LIMIT = 32 * 1024 * 1024
GROUPS = 2
THIRD = 1
SPLIT = 4


def split_table(table):
    high = np.asarray(table, np.float32).astype(jnp.bfloat16)
    low = (np.asarray(table, np.float64) - high.astype(np.float64)).astype(np.float32)
    return high, low.astype(jnp.bfloat16)


def window_tables(count):
    half = WIN // 2 + 1
    unit = 2.0 * np.pi / WIN
    index = np.arange(WIN)
    shifts = np.arange(DISP) - DISP // 2
    turn = unit * np.outer(index, index)
    cos_full, sin_full = np.cos(turn), np.sin(turn)
    rows_y = -(-2 * half // 8) * 8
    first = np.zeros((rows_y, WIN))
    first[0 : 2 * half : 2] = cos_full[:half]
    first[1 : 2 * half : 2] = -sin_full[:half]
    high, low = split_table(first)
    table_y = np.concatenate([high, high, low], axis=1)
    second = np.block([[cos_full, sin_full], [-sin_full, cos_full]])
    high, low = split_table(second)
    table_x = np.concatenate([high, high, low], axis=1)
    third = np.zeros((2, 2, WIN, 2, 2, WIN))
    for e in range(2):
        third[0, e, :, e, 0] = cos_full
        third[1, e, :, e, 0] = sin_full
        third[0, e, :, e, 1] = -sin_full
        third[1, e, :, e, 1] = cos_full
    high, low = split_table(third.reshape(4 * WIN, 4 * WIN))
    table_z = np.concatenate([high, high, low], axis=0)
    part = unit * np.outer(index, shifts)
    cos_part, sin_part = np.cos(part), np.sin(part)
    fourth = np.zeros((4, WIN, 2 * WIN))
    fourth[..., :DISP] = np.stack([cos_part, cos_part, -sin_part, sin_part])
    fourth[..., DISP : 2 * DISP] = np.stack([sin_part, sin_part, cos_part, -cos_part])
    fourth = fourth.reshape(4 * WIN, 2 * WIN)
    shifted = np.stack([np.roll(fourth, w * 2 * DISP, axis=1) for w in range(count)])
    high, low = split_table(shifted)
    table_iz = np.concatenate([high, high, low], axis=1)
    high, low = split_table(np.concatenate([cos_part.T, sin_part.T], axis=1))
    table_ix = np.concatenate([high, high, low], axis=1)
    weight = np.full(half, 2.0)
    weight[0] = weight[-1] = 1.0
    pad = -(-half // 16) * 16
    last = np.zeros((2 * DISP, pad))
    last[:DISP, :half] = cos_part.T[:, :half] * weight
    last[DISP:, :half] = sin_part.T[:, :half] * weight
    high, low = split_table(last)
    table_iy = np.concatenate([high, high, low], axis=1)
    return table_y, table_x, table_z, table_iz, table_ix, table_iy


def halves(value):
    high = value.astype(jnp.bfloat16)
    low = (value - high.astype(jnp.float32)).astype(jnp.bfloat16)
    return high, low


def stacked(value):
    high, low = halves(value)
    return jnp.concatenate([high, low, high], axis=0)


def mul(left, right):
    return jnp.dot(left, right, preferred_element_type=jnp.float32)


def decode(level_ref, target_ref):
    exposures, columns = target_ref.shape[:2]
    for e in range(exposures):
        scale = level_ref[e, columns:, :].astype(jnp.int32).astype(jnp.float32)
        least, width = scale[:1] / GRAIN, scale[1:2]
        step = width / (GRAIN * LEVELS)
        base = least + MIDDLE * step
        present = jnp.where(width > 0.0, 1.0, 0.0)
        for start in range(0, columns, columns // 4):
            place = slice(start, start + columns // 4)
            level = level_ref[e, place, :].astype(jnp.int32).astype(jnp.float32)
            target_ref[e, place, :] = jnp.exp(level * step + base) * present


def first_stage(ext, brick_of, start, mean, table, spectrum_ref):
    half_win = WIN // 2
    _, sy, sz = start
    lane = lax.broadcasted_iota(jnp.int32, (WIN, 2 * WIN), 1)
    row = lax.broadcasted_iota(jnp.int32, (half_win, 2 * WIN), 0)
    left_lane = lane < WIN
    keep = (left_lane & (lane >= sz)) | (~left_lane & (lane < sz + WIN))
    below = row >= sy

    def fold(x):
        brick = brick_of(x)
        inner = pl.ds(pl.multiple_of(x * half_win, half_win), half_win)
        values = []
        for e in range(2):
            low, high = ext[brick, e, inner], ext[brick + 2, e, inner]
            same = ext[brick + 1, e, inner]
            values.append(jnp.concatenate([jnp.where(below, low, high), same], axis=0))
        stay = jnp.where(left_lane, values[0], values[1])
        move = jnp.where(left_lane, values[1], values[0])
        return jnp.where(keep, stay, pltpu.roll(move, WIN, 1)) - mean

    def one_group(i, sums):
        total, square = sums
        for g in range(GROUPS):
            begin = (i * GROUPS + g) * 8
            results = []
            for j in range(0, 8, 2):
                values = [fold(begin + j + k) for k in range(2)]
                for value in values:
                    total = total + value
                    square = square + value * value
                result = mul(table, stacked(jnp.concatenate(values, axis=1)))
                results += [result[:, : 2 * WIN], result[:, 2 * WIN :]]
            spectrum_ref[:, pl.ds(pl.multiple_of(begin, 8), 8), :] = jnp.swapaxes(
                jnp.stack(results), 0, 1
            )
        return total, square

    zero = jnp.zeros((WIN, 2 * WIN), jnp.float32)
    total, square = lax.fori_loop(0, half_win // (8 * GROUPS), one_group, (zero, zero))
    return [jnp.sum(value, axis=0, keepdims=True) for value in (total, square)]


def by_exposure(value):
    left = lax.broadcasted_iota(jnp.int32, value.shape, 1) < WIN
    return (
        jnp.sum(jnp.where(left, value, 0.0), axis=1, keepdims=True),
        jnp.sum(jnp.where(left, 0.0, value), axis=1, keepdims=True),
    )


def middle_body(count, starts, own, near, far, t_y, spectrum_out, stats_out, ext, levels, sems):
    copies = [
        pltpu.make_async_copy(source, target, sems.at[i])
        for i, (source, target) in enumerate(
            [(own, ext.at[1]), (near, levels.at[0]), (far, levels.at[1])]
        )
    ]
    for copy in copies:
        copy.start()
    for copy in copies:
        copy.wait()
    decode(levels.at[0], ext.at[0])
    decode(levels.at[1], ext.at[2])
    exposures, columns, depth = ext.shape[1:]
    sums = [jnp.sum(ext[1, e], axis=0, keepdims=True) for e in range(exposures)]
    lane = lax.broadcasted_iota(jnp.int32, (1, depth), 1)

    def one_window(w, done):
        start = [starts[w, n] for n in range(3)]
        inside = (lane >= start[2]) & (lane < start[2] + WIN)
        means = [
            jnp.sum(jnp.where(inside, value, 0.0), axis=1, keepdims=True) / (columns * WIN)
            for value in sums
        ]
        mean = jnp.where(lane < WIN, means[0], means[1])
        total, square = first_stage(
            ext, lambda x: 0, start, mean, t_y[...], spectrum_out.at[w]
        )
        spare = jnp.zeros((5, depth), jnp.float32)
        stats_out[w] = jnp.concatenate([mean, total, square, spare], axis=0)
        return done

    lax.fori_loop(0, count, one_window, 0)


def window_body(count, starts, stats, *refs):
    middle, left, right, left_near, left_far, right_near, right_far = refs[:7]
    t_y, t_x, t_z, t_iz, t_ix, t_iy, out = refs[7:14]
    ext, levels, sems, spectrum, high_ref, low_ref, product, turned = refs[14:]
    half = WIN // 2 + 1
    pad = t_iy.shape[1] // 3
    sources = [left_near, left, left_far, right_near, right, right_far]
    copies = [
        pltpu.make_async_copy(source, levels.at[i], sems.at[i])
        for i, source in enumerate(sources)
    ]

    def middle_copy(w):
        target = spectrum.at[:, pl.ds(WIN // 2, WIN // 2), :]
        return pltpu.make_async_copy(middle.at[w], target, sems.at[len(sources)])

    middle_copy(0).start()
    for copy in copies:
        copy.start()
    product[...] = jnp.zeros_like(product)
    turned[...] = jnp.zeros_like(turned)
    for copy in copies:
        copy.wait()

    def decode_one(i, done):
        decode(levels.at[i], ext.at[i])
        return done

    lax.fori_loop(0, len(sources), decode_one, 0)
    lane = lax.broadcasted_iota(jnp.int32, (WIN, 2 * WIN), 1)

    def one_window(w, carry):
        start = [starts[w, n] for n in range(3)]
        known = stats[w]
        total, square = first_stage(
            ext,
            lambda x: jnp.where(x >= start[0], 0, 3),
            start,
            known[:1],
            t_y[...],
            spectrum,
        )
        scale = 1.0 / WIN**3
        totals, squares = by_exposure(total + known[1:2]), by_exposure(square + known[2:3])
        powers = [
            square * scale - (total * scale) * (total * scale)
            for total, square in zip(totals, squares)
        ]
        norm = jnp.sqrt(powers[0] + 1e-06) * jnp.sqrt(powers[1] + 1e-06)
        factor = 1.0 / (WIN**3 * WIN**1.5) / norm
        middle_copy(w).wait()

        def second(i, done):
            for j in range(0, 11, 2):
                width = min(2, 11 - j)
                k = i * 11 + j
                values = [
                    spectrum[pl.ds(2 * (k + n), 2)].reshape(2 * WIN, 2 * WIN) for n in range(width)
                ]
                result = mul(t_x[...], stacked(jnp.concatenate(values, axis=1)))
                for n in range(width):
                    part = result[:, 2 * WIN * n : 2 * WIN * (n + 1)]
                    part = jnp.concatenate([part[:WIN], part[WIN:]], axis=1)
                    place = pl.ds(pl.multiple_of((k + n) * WIN, WIN), WIN)
                    high_ref[place, :], low_ref[place, :] = halves(part)
            return done

        lax.fori_loop(0, half // 11, second, 0)

        @pl.when(w + 1 < count)
        def _():
            middle_copy(w + 1).start()

        block = half * WIN // (THIRD * SPLIT)

        def third(i, done):
            for g in range(SPLIT):
                place = pl.ds(pl.multiple_of((i * SPLIT + g) * block, block), block)
                high, low = high_ref[place, :], low_ref[place, :]
                value = mul(jnp.concatenate([high, low, high], axis=1), t_z[...])
                one, two = value[:, : 2 * WIN] * factor, value[:, 2 * WIN :]
                if g == 0:
                    row = lax.broadcasted_iota(jnp.int32, one.shape, 0)
                    column = lax.broadcasted_iota(jnp.int32, one.shape, 1)
                    one = jnp.where((i * block + row == 0) & (column % WIN == 0), 0.0, one)
                cross = jnp.concatenate([one * two, one * pltpu.roll(two, WIN, 1)], axis=1)
                high, low = halves(cross)
                product[place, :] += mul(jnp.concatenate([high, low, high], axis=1), t_iz[w])
            return done

        lax.fori_loop(0, THIRD, third, 0)
        return carry

    lax.fori_loop(0, count, one_window, 0)

    real_lane = lane % (2 * DISP) < DISP

    def fifth(i, done):
        for j in range(11):
            k = i * 11 + j
            value = product[pl.ds(pl.multiple_of(k * WIN, WIN), WIN), :]
            turn = jnp.where(
                real_lane, -pltpu.roll(value, 2 * WIN - DISP, 1), pltpu.roll(value, DISP, 1)
            )
            value = jnp.concatenate([value, turn], axis=0)
            turned[pl.ds(k, DISP, stride=pad), :] = mul(t_ix[...], stacked(value))
        return done

    lax.fori_loop(0, half // 11, fifth, 0)
    for d in range(DISP):
        value = mul(t_iy[...], stacked(turned[d * pad : (d + 1) * pad, :]))
        out[:, d * 2 * WIN : (d + 1) * 2 * WIN] = value[:DISP] - pltpu.roll(
            value[DISP:], 2 * WIN - DISP, 1
        )


def middle_spectra(own, near, far, starts):
    count = starts.shape[0]
    table = window_tables(count)[0]
    vmem = pl.BlockSpec(memory_space=pltpu.VMEM)
    anywhere = pl.BlockSpec(memory_space=pl.ANY)
    return pl.pallas_call(
        functools.partial(middle_body, count),
        out_shape=[
            jax.ShapeDtypeStruct((count, table.shape[0], WIN // 2, 2 * WIN), jnp.float32),
            jax.ShapeDtypeStruct((count, 8, 2 * WIN), jnp.float32),
        ],
        in_specs=[pl.BlockSpec(memory_space=pltpu.SMEM), anywhere, anywhere, anywhere, vmem],
        out_specs=[vmem, vmem],
        scratch_shapes=[
            pltpu.VMEM((3,) + own.shape, jnp.float32),
            pltpu.VMEM((2,) + near.shape, jnp.int16),
            pltpu.SemaphoreType.DMA((3,)),
        ],
        compiler_params=pltpu.CompilerParams(vmem_limit_bytes=LIMIT),
        name="middle",
    )(starts, own, near, far, jnp.asarray(table))


def window_correlations(own, bricks, starts):
    left, right, near, far, *corners = bricks
    middle, stats = middle_spectra(own, near, far, starts)
    bricks = [left, right, *corners]
    count = starts.shape[0]
    tables = window_tables(count)
    half = WIN // 2 + 1
    rows_y = tables[0].shape[0]
    pad = tables[5].shape[1] // 3
    vmem = pl.BlockSpec(memory_space=pltpu.VMEM)
    result = pl.pallas_call(
        functools.partial(window_body, count),
        out_shape=jax.ShapeDtypeStruct((DISP, DISP * 2 * WIN), jnp.float32),
        in_specs=[pl.BlockSpec(memory_space=pltpu.SMEM), vmem]
        + [pl.BlockSpec(memory_space=pl.ANY)] * 7
        + [vmem] * 6,
        out_specs=vmem,
        scratch_shapes=[
            pltpu.VMEM((6,) + own.shape, jnp.float32),
            pltpu.VMEM((6,) + left.shape, jnp.int16),
            pltpu.SemaphoreType.DMA((7,)),
            pltpu.VMEM((rows_y, WIN, 2 * WIN), jnp.float32),
            pltpu.VMEM((half * WIN, 4 * WIN), jnp.bfloat16),
            pltpu.VMEM((half * WIN, 4 * WIN), jnp.bfloat16),
            pltpu.VMEM((half * WIN, 2 * WIN), jnp.float32),
            pltpu.VMEM((DISP * pad, 2 * WIN), jnp.float32),
        ],
        compiler_params=pltpu.CompilerParams(vmem_limit_bytes=WIDE_LIMIT),
        name="windows",
    )(starts, stats, middle, *bricks, *[jnp.asarray(t) for t in tables])
    result = result.reshape(DISP, DISP, 2 * WIN // (2 * DISP), 2 * DISP)[:, :, :count, :DISP]
    return result.transpose(2, 1, 0, 3).reshape(count, DISP**3)


LANES = 128


def chosen_products(value, member, weights_ref):
    count = weights_ref.shape[1]
    half_count = count // 2
    size = weights_ref.shape[2]
    copies = value.shape[0] // member.shape[0]
    total = None
    for start in range(0, half_count, TERMS):
        picked, tables = [], []
        for j in range(start, min(start + TERMS, half_count)):
            hit = (member == j) | (member == j + half_count)
            hit = jnp.concatenate([hit] * copies, axis=0)
            picked.append(jnp.where(hit, value, jnp.zeros_like(value)))
            tables.append(
                jnp.concatenate([weights_ref[0, j], weights_ref[0, j + half_count]], axis=1)
            )
        term = mul(jnp.concatenate(picked, axis=1), jnp.concatenate(tables, axis=0))
        total = term if total is None else total + term
    upper = jnp.concatenate([member.astype(jnp.float32)] * copies, axis=0) >= half_count
    return jnp.where(upper, total[:, size:], total[:, :size])


def placed_tiles(tile, count):
    columns = lax.broadcasted_iota(jnp.int32, tile.shape, 1).astype(jnp.float32)
    columns = columns.astype(tile.dtype)
    one, zero = jnp.ones_like(tile), jnp.zeros_like(tile)
    parts = [
        jnp.where(tile - start == columns, one, zero) for start in range(0, count, LANES)
    ]
    return jnp.concatenate(parts, axis=1)[:, :count]


def sweep_body(back, forward, parity_ref, *refs):
    refs = list(refs)
    volume_ref = refs.pop(0)
    if back:
        own_ratio, other_ratio, back_tile, back_member, back_weights = refs[:5]
        refs = refs[5:]
    if forward:
        next_row, next_member, next_weights = refs[:3]
        refs = refs[3:]
    if back:
        volume_out = refs.pop(0)
    exposures, columns, depth = volume_ref.shape
    block = columns // STEPS
    odd = parity_ref[0] == 1
    if back:
        own, other = own_ratio[...], other_ratio[...]
        ratios = [jnp.where(odd, other, own), jnp.where(odd, own, other)]
        ratios = jnp.concatenate(ratios, axis=1)
    tiles = refs[0].shape[0]

    def one_block(i, total):
        place = pl.ds(pl.multiple_of(i * block, block), block)
        volume = volume_ref[:, place, :].reshape(exposures * block, depth)
        if back:
            placement = placed_tiles(back_tile[0, place, :], own.shape[0])
            spread = mul(placement, ratios).astype(jnp.bfloat16)
            spread = jnp.concatenate(
                [spread[:, e * LANES : (e + 1) * LANES] for e in range(exposures)], axis=0
            )
            member = back_member[0, place, :]
            volume = volume * jnp.exp(chosen_products(spread, member, back_weights))
            volume_out[:, place, :] = volume.reshape(exposures, block, depth)
        if forward:
            member = next_member[0, place, :]
            projected = chosen_products(volume.astype(jnp.bfloat16), member, next_weights)
            parts = list(halves(projected))
            parts = [p[e * block : (e + 1) * block] for p in parts for e in range(exposures)]
            rows = lax.broadcasted_iota(jnp.int32, (tiles, block), 0)
            hit = next_row[0, pl.ds(i, 1), :] == rows
            placement = jnp.where(hit, 1.0, 0.0).astype(jnp.bfloat16)
            value = mul(placement, jnp.concatenate(parts, axis=1))
            size = value.shape[1] // 2
            total = total + (value[:, :size] + value[:, size:])
        return total

    if forward:
        start = jnp.zeros((tiles, exposures * depth), jnp.float32)
        if UNROLL:
            for i in range(STEPS):
                start = one_block(i, start)
            total = start
        else:
            total = lax.fori_loop(0, STEPS, one_block, start)
        kept_ref, sent_ref = refs
        first, second = total[:, :depth], total[:, depth:]
        kept_ref[...] = jnp.where(odd, second, first)
        sent_ref[...] = jnp.where(odd, first, second)
    else:
        lax.fori_loop(0, STEPS, one_block, 0)
        (code_ref,) = refs
        for e in range(exposures):
            logs = jnp.log(jnp.maximum(volume_out[e], 1e-37))
            least = jnp.floor(jnp.min(logs, axis=0, keepdims=True) * GRAIN)
            width = jnp.floor(jnp.max(logs, axis=0, keepdims=True) * GRAIN - least) + 1.0
            rate = (GRAIN * LEVELS) / width
            level = jnp.floor((logs - least / GRAIN) * rate + 0.5) - MIDDLE
            code_ref[e, :columns, :] = level.astype(jnp.int32).astype(jnp.int16)
            row = lax.broadcasted_iota(jnp.int32, (SPARE, depth), 0)
            extra = jnp.where(row == 0, least, jnp.where(row == 1, width, 0.0))
            code_ref[e, columns:, :] = extra.astype(jnp.int32).astype(jnp.int16)


def sweep_step(parity, volume, ratios, columns, weights, weights_turned, tiles, camera, following):
    exposures, count, depth = volume.shape
    pixels = weights.shape[2]
    back, forward = camera is not None, following is not None
    rows, tile_values, members = columns

    def taken(value, index):
        shape = (1,) + value.shape[1:]
        return pl.BlockSpec(shape, lambda i: (index,) + (0,) * (len(shape) - 1))

    def whole(shape):
        return pl.BlockSpec(shape, lambda i: (0,) * len(shape))

    operands = [parity, volume]
    specs = [pl.BlockSpec(memory_space=pltpu.SMEM), whole(volume.shape)]
    shapes = []
    if back:
        operands += [*ratios, tile_values, members, weights]
        specs += [whole((tiles, pixels))] * 2
        specs += [taken(tile_values, camera), taken(members, camera), taken(weights, camera)]
        shapes.append(jax.ShapeDtypeStruct(volume.shape, jnp.float32))
    if forward:
        operands += [rows, members, weights_turned]
        specs += [taken(value, following) for value in operands[-3:]]
        shapes += [jax.ShapeDtypeStruct((tiles, pixels), jnp.float32)] * 2
    else:
        shapes.append(jax.ShapeDtypeStruct((exposures, count + SPARE, depth), jnp.int16))
    result = pl.pallas_call(
        functools.partial(sweep_body, back, forward),
        grid=(1,),
        in_specs=specs,
        out_specs=[whole(value.shape) for value in shapes],
        out_shape=shapes,
        compiler_params=pltpu.CompilerParams(vmem_limit_bytes=LIMIT),
        name="sweep",
    )(*operands)
    return (result[0] if back else volume), (result[-2:] if forward else result[-1])


def column_tables(target, member):
    shape = target.shape + (LANES,)
    tile_values = jnp.broadcast_to(target.astype(jnp.bfloat16)[..., None], shape)
    members = jnp.broadcast_to(member.astype(jnp.bfloat16)[..., None], shape)
    rows = target.reshape(target.shape[0], STEPS, target.shape[1] // STEPS)
    return rows, tile_values, members


def partner_of(count, bit):
    return [(i, i ^ bit) for i in range(count)]


def shared_ratio(kept, sent, picture):
    count = lax.axis_size("wide")
    pair = partner_of(count, 1)
    total = kept + lax.ppermute(sent, "wide", pair)
    bit = 2
    while bit < count:
        total = total + lax.ppermute(total, "wide", partner_of(count, bit))
        bit *= 2
    ratio = (picture - jnp.log(total + 1.0)).astype(jnp.bfloat16)
    return ratio, lax.ppermute(ratio, "wide", pair)


def reconstructed(initial, images, blocks, lib_index, tile_map):
    count = lax.axis_size("wide")
    own_index = lax.axis_index("wide")
    exposures, brick_x, brick_y, depth = initial.shape
    cameras, tile_rows, tile_cols, pixels = images.shape[1:]
    tile_count = tile_rows * tile_cols
    tiles = count * tile_count
    columns = brick_x * brick_y
    strip = own_index - count // 2 + tile_map // tile_count
    target = strip * tile_count + tile_map % tile_count
    missing = -(-tiles // LANES) * LANES
    target = jnp.where((strip >= 0) & (strip < count), target, missing)
    tables = column_tables(
        target.reshape(cameras, columns), lib_index.reshape(cameras, columns)
    )
    parity = (own_index % 2).reshape(1)
    pictures = jnp.log(images.reshape(exposures, cameras, tile_count, pixels) + 1.0)
    by_core = jnp.broadcast_to(pictures[None], (count // 2,) + pictures.shape)
    by_core = by_core.reshape((count, cameras, tile_count, pixels))
    gathered = lax.all_to_all(by_core, "wide", split_axis=0, concat_axis=0, tiled=True)
    gathered = gathered.transpose(1, 0, 2, 3).reshape(cameras, tiles, pixels)
    turned = blocks.transpose(0, 1, 3, 2)
    volume = initial.reshape(exposures, columns, depth)
    order = [camera for _ in range(SWEEPS) for camera in range(cameras)]
    step = functools.partial(
        sweep_step, columns=tables, weights=blocks, weights_turned=turned, tiles=tiles
    )
    volume, partial_value = step(parity, volume, None, camera=None, following=order[0])
    for place, camera in enumerate(order):
        following = order[place + 1] if place + 1 < len(order) else None
        ratios = shared_ratio(*partial_value, gathered[camera])
        volume, partial_value = step(parity, volume, ratios, camera=camera, following=following)
    return volume, partial_value


def neighbours(own):
    def shifted(value, axis, step):
        count = lax.axis_size(axis)
        pairs = [(i, i + step) for i in range(count) if 0 <= i + step < count]
        return lax.ppermute(value, axis, pairs)

    near = shifted(own, "narrow", 1)
    right = shifted(own, "wide", -1)
    far = shifted(own, "narrow", -1)
    left = shifted(own, "wide", 1)
    left_near = shifted(near, "wide", 1)
    right_near = shifted(right, "narrow", 1)
    left_far = shifted(far, "wide", 1)
    right_far = shifted(right, "narrow", -1)
    return [left, right, near, far, left_near, left_far, right_near, right_far]


def body(initial, images, blocks, lib_index, tile_map, win_x, win_y, win_z):
    volume, code = reconstructed(initial, images, blocks, lib_index, tile_map)
    starts = jnp.stack([win_x.reshape(-1), win_y.reshape(-1), win_z.reshape(-1)], axis=1)
    correlation = window_correlations(volume, neighbours(code), starts)
    return (volume.reshape(initial.shape), correlation.reshape(1, 1, starts.shape[0], DISP * DISP * DISP))


def solution(mesh):
    placed = (
        P(None, "wide", "narrow", None),
        P(None, None, "wide", "narrow", None),
        P(),
        P(None, "wide", "narrow"),
        P(None, "wide", "narrow"),
        P("wide", "narrow", None),
        P("wide", "narrow", None),
        P("wide", "narrow", None),
    )
    return jax.shard_map(
        body,
        mesh=mesh,
        in_specs=placed,
        out_specs=(P(None, "wide", "narrow", None), P("wide", "narrow", None, None)),
        check_vma=False,
    )
```

profile of v0, /device:TPU:0, one launch (start us, length us, event | category | flops | bytes accessed | tf_op | source)
XLA Modules:
  0.0 202.8 jit_solution(12427534503529025997)
XLA Ops:
  2.3 5.3 %all-to-all-start = ((f32[8,4,18,128]{3,1,2,0:T(4,128)}), f32[8,4,18,128]{3,1,2,0:T(4,128)S(1)}, u32[]{:S(2)}, u32[]{:S(2)}) async-start(f32[8,4,18,128]{3,1,2,0:T(4,128)} %bitcast.3), calls=%async_computation | async-start | bytes 589824 | tf_op jit(solution)/shard_map/all_to_all | solution.py:555
  18.4 2.7 %collective-permute-done.1 = f32[144,128]{1,0:T(8,128)S(1)} collective-permute-done((f32[144,128]{1,0:T(8,128)S(1)}, f32[144,128]{1,0:T(8,128)S(1)}, u32[]{:S(2)}, u32[]{:S(2)}) %collective-permute-start.1) | collective-permute-done | bytes 73760 | tf_op jit(solution)/shard_map/ppermute | solution.py:530
  36.1 2.7 %collective-permute-done.5 = f32[144,128]{1,0:T(8,128)S(1)} collective-permute-done((f32[144,128]{1,0:T(8,128)S(1)}, f32[144,128]{1,0:T(8,128)S(1)}, u32[]{:S(2)}, u32[]{:S(2)}) %collective-permute-start.5) | collective-permute-done | bytes 73760 | tf_op jit(solution)/shard_map/ppermute | solution.py:530
  40.5 2.7 %collective-permute-done.6 = f32[144,128]{1,0:T(8,128)S(1)} collective-permute-done((f32[144,128]{1,0:T(8,128)S(1)}, f32[144,128]{1,0:T(8,128)S(1)}, u32[]{:S(2)}, u32[]{:S(2)}) %collective-permute-start.6) | collective-permute-done | bytes 73760 | tf_op jit(solution)/shard_map/ppermute | solution.py:530
  50.1 2.7 %collective-permute-done.9 = f32[144,128]{1,0:T(8,128)S(1)} collective-permute-done((f32[144,128]{1,0:T(8,128)S(1)}, f32[144,128]{1,0:T(8,128)S(1)}, u32[]{:S(2)}, u32[]{:S(2)}) %collective-permute-start.9) | collective-permute-done | bytes 73760 | tf_op jit(solution)/shard_map/ppermute | solution.py:530
  54.6 2.7 %collective-permute-done.10 = f32[144,128]{1,0:T(8,128)S(1)} collective-permute-done((f32[144,128]{1,0:T(8,128)S(1)}, f32[144,128]{1,0:T(8,128)S(1)}, u32[]{:S(2)}, u32[]{:S(2)}) %collective-permute-start.10) | collective-permute-done | bytes 73760 | tf_op jit(solution)/shard_map/ppermute | solution.py:530
  64.2 2.7 %collective-permute-done.13 = f32[144,128]{1,0:T(8,128)S(1)} collective-permute-done((f32[144,128]{1,0:T(8,128)S(1)}, f32[144,128]{1,0:T(8,128)S(1)}, u32[]{:S(2)}, u32[]{:S(2)}) %collective-permute-start.13) | collective-permute-done | bytes 73760 | tf_op jit(solution)/shard_map/ppermute | solution.py:530
  68.6 2.7 %collective-permute-done.14 = f32[144,128]{1,0:T(8,128)S(1)} collective-permute-done((f32[144,128]{1,0:T(8,128)S(1)}, f32[144,128]{1,0:T(8,128)S(1)}, u32[]{:S(2)}, u32[]{:S(2)}) %collective-permute-start.14) | collective-permute-done | bytes 73760 | tf_op jit(solution)/shard_map/ppermute | solution.py:530
  72.6 2.7 %sweep.13 = (f32[2,1024,128]{2,1,0:T(8,128)S(1)}, f32[144,128]{1,0:T(8,128)S(1)}, f32[144,128]{1,0:T(8,128)S(1)}) custom-call(s32[1]{0:T(128)} %bitcast.parity_ref, f32[2,1024,128]{2,1,0:T(8,128)S(1)} %get-tuple-element.37.refs_0_, bf16[144,128]{1,0:T(8,128)(2,1)S(1)} %subtract_convert_fusion.4.refs_1_, ...), custom_call_target="tpu_custom_call" | custom-call | tf_op jit(solution)/shard_map/sweep/pallas_call | solution.py:500
  78.4 2.7 %collective-permute-done.17 = f32[144,128]{1,0:T(8,128)S(1)} collective-permute-done((f32[144,128]{1,0:T(8,128)S(1)}, f32[144,128]{1,0:T(8,128)S(1)}, u32[]{:S(2)}, u32[]{:S(2)}) %collective-permute-start.17) | collective-permute-done | bytes 73760 | tf_op jit(solution)/shard_map/ppermute | solution.py:530
  82.9 2.7 %collective-permute-done.18 = f32[144,128]{1,0:T(8,128)S(1)} collective-permute-done((f32[144,128]{1,0:T(8,128)S(1)}, f32[144,128]{1,0:T(8,128)S(1)}, u32[]{:S(2)}, u32[]{:S(2)}) %collective-permute-start.18) | collective-permute-done | bytes 73760 | tf_op jit(solution)/shard_map/ppermute | solution.py:530
  92.5 2.7 %collective-permute-done.21 = f32[144,128]{1,0:T(8,128)S(1)} collective-permute-done((f32[144,128]{1,0:T(8,128)S(1)}, f32[144,128]{1,0:T(8,128)S(1)}, u32[]{:S(2)}, u32[]{:S(2)}) %collective-permute-start.21) | collective-permute-done | bytes 73760 | tf_op jit(solution)/shard_map/ppermute | solution.py:530
  96.9 2.7 %collective-permute-done.22 = f32[144,128]{1,0:T(8,128)S(1)} collective-permute-done((f32[144,128]{1,0:T(8,128)S(1)}, f32[144,128]{1,0:T(8,128)S(1)}, u32[]{:S(2)}, u32[]{:S(2)}) %collective-permute-start.22) | collective-permute-done | bytes 73760 | tf_op jit(solution)/shard_map/ppermute | solution.py:530
  106.6 2.7 %collective-permute-done.25 = f32[144,128]{1,0:T(8,128)S(1)} collective-permute-done((f32[144,128]{1,0:T(8,128)S(1)}, f32[144,128]{1,0:T(8,128)S(1)}, u32[]{:S(2)}, u32[]{:S(2)}) %collective-permute-start.25) | collective-permute-done | bytes 73760 | tf_op jit(solution)/shard_map/ppermute | solution.py:530
  111.0 2.7 %collective-permute-done.26 = f32[144,128]{1,0:T(8,128)S(1)} collective-permute-done((f32[144,128]{1,0:T(8,128)S(1)}, f32[144,128]{1,0:T(8,128)S(1)}, u32[]{:S(2)}, u32[]{:S(2)}) %collective-permute-start.26) | collective-permute-done | bytes 73760 | tf_op jit(solution)/shard_map/ppermute | solution.py:530
  125.1 2.7 %collective-permute-done.30 = f32[144,128]{1,0:T(8,128)S(1)} collective-permute-done((f32[144,128]{1,0:T(8,128)S(1)}, f32[144,128]{1,0:T(8,128)S(1)}, u32[]{:S(2)}, u32[]{:S(2)}) %collective-permute-start.30) | collective-permute-done | bytes 73760 | tf_op jit(solution)/shard_map/ppermute | solution.py:530
  131.6 4.3 %collective-permute-start.32 = (s16[2,1040,128]{2,1,0:T(8,128)(2,1)}, s16[2,1040,128]{2,1,0:T(8,128)(2,1)}, u32[]{:S(2)}, u32[]{:S(2)}) collective-permute-start(s16[2,1040,128]{2,1,0:T(8,128)(2,1)} %get-tuple-element.53), channel_id=1, source_target_pairs={{0,1},{1,2},{2,3},{4,5},{5,6},{6,7},{8,9},{9,10},{10,11},{12,13},{... | collective-permute-start | bytes 1597448 | tf_op jit(solution)/shard_map/ppermute | solution.py:575
  138.4 3.1 %collective-permute-start.34 = (s16[2,1040,128]{2,1,0:T(8,128)(2,1)}, s16[2,1040,128]{2,1,0:T(8,128)(2,1)S(1)}, u32[]{:S(2)}, u32[]{:S(2)}) collective-permute-start(s16[2,1040,128]{2,1,0:T(8,128)(2,1)} %get-tuple-element.53), channel_id=1, source_target_pairs={{0,4},{4,8},{8,12},{12,16},{16,20},{20,24},{24,28},{1,5},{5,9},{9,... | collective-permute-start | bytes 1597448 | tf_op jit(solution)/shard_map/ppermute | solution.py:575
  141.5 5.5 %collective-permute-done.32.near = s16[2,1040,128]{2,1,0:T(8,128)(2,1)} collective-permute-done((s16[2,1040,128]{2,1,0:T(8,128)(2,1)}, s16[2,1040,128]{2,1,0:T(8,128)(2,1)}, u32[]{:S(2)}, u32[]{:S(2)}) %collective-permute-start.32) | collective-permute-done | bytes 532512 | tf_op jit(solution)/shard_map/ppermute | solution.py:575
  148.6 3.4 %collective-permute-done.33.far = s16[2,1040,128]{2,1,0:T(8,128)(2,1)} collective-permute-done((s16[2,1040,128]{2,1,0:T(8,128)(2,1)}, s16[2,1040,128]{2,1,0:T(8,128)(2,1)}, u32[]{:S(2)}, u32[]{:S(2)}) %collective-permute-start.33) | collective-permute-done | bytes 532512 | tf_op jit(solution)/shard_map/ppermute | solution.py:575
  153.2 4.9 %collective-permute-start.38 = (s16[2,1040,128]{2,1,0:T(8,128)(2,1)S(1)}, s16[2,1040,128]{2,1,0:T(8,128)(2,1)}, u32[]{:S(2)}, u32[]{:S(2)}) collective-permute-start(s16[2,1040,128]{2,1,0:T(8,128)(2,1)S(1)} %collective-permute-done.35.refs_2_), channel_id=1, source_target_pairs={{0,1},{1,2},{2,3},{4,5},{5,6},{6,7},{8,9},{9,10},{10,11},{12,13},{... | collective-permute-start | bytes 1597448 | tf_op jit(solution)/shard_map/ppermute | solution.py:575
  162.3 6.6 %middle.1 = (f32[4,72,32,128]{3,2,1,0:T(8,128)S(1)}, f32[4,8,128]{2,1,0:T(8,128)S(1)}) custom-call(s32[4,3]{1,0:T(4,128)S(1)} %pad_add_fusion.starts, f32[2,1024,128]{2,1,0:T(8,128)S(1)} %copy-done.3, s16[2,1040,128]{2,1,0:T(8,128)(2,1)} %collective-permute-done.32.near, s16[2,1040,128]{2,1,0:T(8,128)(2,1)} %collective-permute-done.33.far, ...), custom_call_target="tpu_custom_call" | custom-call | tf_op jit(solution)/shard_map/middle/pallas_call | solution.py:315
  169.7 5.2 %collective-permute-done.39.refs_6_ = s16[2,1040,128]{2,1,0:T(8,128)(2,1)} collective-permute-done((s16[2,1040,128]{2,1,0:T(8,128)(2,1)S(1)}, s16[2,1040,128]{2,1,0:T(8,128)(2,1)}, u32[]{:S(2)}, u32[]{:S(2)}) %collective-permute-start.39) | collective-permute-done | bytes 532512 | tf_op jit(solution)/shard_map/ppermute | solution.py:575
  177.3 24.0 %windows.1 = f32[16,2048]{1,0:T(8,128)S(1)} custom-call(s32[4,3]{1,0:T(4,128)S(1)} %pad_add_fusion.starts, f32[4,8,128]{2,1,0:T(8,128)S(1)} %get-tuple-element.54.stats, f32[4,72,32,128]{3,2,1,0:T(8,128)S(1)} %get-tuple-element.55.refs_0_, s16[2,1040,128]{2,1,0:T(8,128)(2,1)S(1)} %collective-permute-done.34.refs_1_, ...), custom_call_target="tpu_custom_call" | custom-call | tf_op jit(solution)/shard_map/windows/pallas_call | solution.py:343
  (146 shorter events, 99.7 us)
Async XLA Ops:
  2.3 21.1 %all-to-all-start = ((f32[8,4,18,128]{3,1,2,0:T(4,128)}), f32[8,4,18,128]{3,1,2,0:T(4,128)S(1)}, u32[]{:S(2)}, u32[]{:S(2)}) async-start(f32[8,4,18,128]{3,1,2,0:T(4,128)} %bitcast.3), calls=%async_computation | async-start | bytes 589824 | tf_op jit(solution)/shard_map/all_to_all | solution.py:555
  16.4 4.6 %collective-permute-start.1 = (f32[144,128]{1,0:T(8,128)S(1)}, f32[144,128]{1,0:T(8,128)S(1)}, u32[]{:S(2)}, u32[]{:S(2)}) collective-permute-start(f32[144,128]{1,0:T(8,128)S(1)} %add.135), channel_id=1, source_target_pairs={{0,8},{4,12},{8,0},{12,4},{16,24},{20,28},{24,16},{28,20},{1,9},{5... | collective-permute-start | bytes 221192 | tf_op jit(solution)/shard_map/ppermute | solution.py:530
  21.7 4.7 %collective-permute-start.2 = (f32[144,128]{1,0:T(8,128)}, f32[144,128]{1,0:T(8,128)}, u32[]{:S(2)}, u32[]{:S(2)}) collective-permute-start(f32[144,128]{1,0:T(8,128)} %add.136), channel_id=1, source_target_pairs={{0,16},{4,20},{8,24},{12,28},{16,0},{20,4},{24,8},{28,12},{1,17},{... | collective-permute-start | bytes 221192 | tf_op jit(solution)/shard_map/ppermute | solution.py:530
  34.3 4.4 %collective-permute-start.5 = (f32[144,128]{1,0:T(8,128)S(1)}, f32[144,128]{1,0:T(8,128)S(1)}, u32[]{:S(2)}, u32[]{:S(2)}) collective-permute-start(f32[144,128]{1,0:T(8,128)S(1)} %add.139), channel_id=1, source_target_pairs={{0,8},{4,12},{8,0},{12,4},{16,24},{20,28},{24,16},{28,20},{1,9},{5... | collective-permute-start | bytes 221192 | tf_op jit(solution)/shard_map/ppermute | solution.py:530
  38.8 4.4 %collective-permute-start.6 = (f32[144,128]{1,0:T(8,128)S(1)}, f32[144,128]{1,0:T(8,128)S(1)}, u32[]{:S(2)}, u32[]{:S(2)}) collective-permute-start(f32[144,128]{1,0:T(8,128)S(1)} %add.140), channel_id=1, source_target_pairs={{0,16},{4,20},{8,24},{12,28},{16,0},{20,4},{24,8},{28,12},{1,17},{... | collective-permute-start | bytes 221192 | tf_op jit(solution)/shard_map/ppermute | solution.py:530
  48.4 4.4 %collective-permute-start.9 = (f32[144,128]{1,0:T(8,128)S(1)}, f32[144,128]{1,0:T(8,128)S(1)}, u32[]{:S(2)}, u32[]{:S(2)}) collective-permute-start(f32[144,128]{1,0:T(8,128)S(1)} %add.143), channel_id=1, source_target_pairs={{0,8},{4,12},{8,0},{12,4},{16,24},{20,28},{24,16},{28,20},{1,9},{5... | collective-permute-start | bytes 221192 | tf_op jit(solution)/shard_map/ppermute | solution.py:530
  52.8 4.4 %collective-permute-start.10 = (f32[144,128]{1,0:T(8,128)S(1)}, f32[144,128]{1,0:T(8,128)S(1)}, u32[]{:S(2)}, u32[]{:S(2)}) collective-permute-start(f32[144,128]{1,0:T(8,128)S(1)} %add.144), channel_id=1, source_target_pairs={{0,16},{4,20},{8,24},{12,28},{16,0},{20,4},{24,8},{28,12},{1,17},{... | collective-permute-start | bytes 221192 | tf_op jit(solution)/shard_map/ppermute | solution.py:530
  62.5 4.4 %collective-permute-start.13 = (f32[144,128]{1,0:T(8,128)S(1)}, f32[144,128]{1,0:T(8,128)S(1)}, u32[]{:S(2)}, u32[]{:S(2)}) collective-permute-start(f32[144,128]{1,0:T(8,128)S(1)} %add.147), channel_id=1, source_target_pairs={{0,8},{4,12},{8,0},{12,4},{16,24},{20,28},{24,16},{28,20},{1,9},{5... | collective-permute-start | bytes 221192 | tf_op jit(solution)/shard_map/ppermute | solution.py:530
  66.9 4.4 %collective-permute-start.14 = (f32[144,128]{1,0:T(8,128)S(1)}, f32[144,128]{1,0:T(8,128)S(1)}, u32[]{:S(2)}, u32[]{:S(2)}) collective-permute-start(f32[144,128]{1,0:T(8,128)S(1)} %add.148), channel_id=1, source_target_pairs={{0,16},{4,20},{8,24},{12,28},{16,0},{20,4},{24,8},{28,12},{1,17},{... | collective-permute-start | bytes 221192 | tf_op jit(solution)/shard_map/ppermute | solution.py:530
  76.7 4.4 %collective-permute-start.17 = (f32[144,128]{1,0:T(8,128)S(1)}, f32[144,128]{1,0:T(8,128)S(1)}, u32[]{:S(2)}, u32[]{:S(2)}) collective-permute-start(f32[144,128]{1,0:T(8,128)S(1)} %add.151), channel_id=1, source_target_pairs={{0,8},{4,12},{8,0},{12,4},{16,24},{20,28},{24,16},{28,20},{1,9},{5... | collective-permute-start | bytes 221192 | tf_op jit(solution)/shard_map/ppermute | solution.py:530
  81.1 4.4 %collective-permute-start.18 = (f32[144,128]{1,0:T(8,128)S(1)}, f32[144,128]{1,0:T(8,128)S(1)}, u32[]{:S(2)}, u32[]{:S(2)}) collective-permute-start(f32[144,128]{1,0:T(8,128)S(1)} %add.152), channel_id=1, source_target_pairs={{0,16},{4,20},{8,24},{12,28},{16,0},{20,4},{24,8},{28,12},{1,17},{... | collective-permute-start | bytes 221192 | tf_op jit(solution)/shard_map/ppermute | solution.py:530
  90.7 4.4 %collective-permute-start.21 = (f32[144,128]{1,0:T(8,128)S(1)}, f32[144,128]{1,0:T(8,128)S(1)}, u32[]{:S(2)}, u32[]{:S(2)}) collective-permute-start(f32[144,128]{1,0:T(8,128)S(1)} %add.155), channel_id=1, source_target_pairs={{0,8},{4,12},{8,0},{12,4},{16,24},{20,28},{24,16},{28,20},{1,9},{5... | collective-permute-start | bytes 221192 | tf_op jit(solution)/shard_map/ppermute | solution.py:530
  95.2 4.4 %collective-permute-start.22 = (f32[144,128]{1,0:T(8,128)S(1)}, f32[144,128]{1,0:T(8,128)S(1)}, u32[]{:S(2)}, u32[]{:S(2)}) collective-permute-start(f32[144,128]{1,0:T(8,128)S(1)} %add.156), channel_id=1, source_target_pairs={{0,16},{4,20},{8,24},{12,28},{16,0},{20,4},{24,8},{28,12},{1,17},{... | collective-permute-start | bytes 221192 | tf_op jit(solution)/shard_map/ppermute | solution.py:530
  104.8 4.4 %collective-permute-start.25 = (f32[144,128]{1,0:T(8,128)S(1)}, f32[144,128]{1,0:T(8,128)S(1)}, u32[]{:S(2)}, u32[]{:S(2)}) collective-permute-start(f32[144,128]{1,0:T(8,128)S(1)} %add.159), channel_id=1, source_target_pairs={{0,8},{4,12},{8,0},{12,4},{16,24},{20,28},{24,16},{28,20},{1,9},{5... | collective-permute-start | bytes 221192 | tf_op jit(solution)/shard_map/ppermute | solution.py:530
  109.2 4.4 %collective-permute-start.26 = (f32[144,128]{1,0:T(8,128)S(1)}, f32[144,128]{1,0:T(8,128)S(1)}, u32[]{:S(2)}, u32[]{:S(2)}) collective-permute-start(f32[144,128]{1,0:T(8,128)S(1)} %add.160), channel_id=1, source_target_pairs={{0,16},{4,20},{8,24},{12,28},{16,0},{20,4},{24,8},{28,12},{1,17},{... | collective-permute-start | bytes 221192 | tf_op jit(solution)/shard_map/ppermute | solution.py:530
  118.9 4.4 %collective-permute-start.29 = (f32[144,128]{1,0:T(8,128)S(1)}, f32[144,128]{1,0:T(8,128)S(1)}, u32[]{:S(2)}, u32[]{:S(2)}) collective-permute-start(f32[144,128]{1,0:T(8,128)S(1)} %add.163), channel_id=1, source_target_pairs={{0,8},{4,12},{8,0},{12,4},{16,24},{20,28},{24,16},{28,20},{1,9},{5... | collective-permute-start | bytes 221192 | tf_op jit(solution)/shard_map/ppermute | solution.py:530
  131.6 15.5 %collective-permute-start.32 = (s16[2,1040,128]{2,1,0:T(8,128)(2,1)}, s16[2,1040,128]{2,1,0:T(8,128)(2,1)}, u32[]{:S(2)}, u32[]{:S(2)}) collective-permute-start(s16[2,1040,128]{2,1,0:T(8,128)(2,1)} %get-tuple-element.53), channel_id=1, source_target_pairs={{0,1},{1,2},{2,3},{4,5},{5,6},{6,7},{8,9},{9,10},{10,11},{12,13},{... | collective-permute-start | bytes 1597448 | tf_op jit(solution)/shard_map/ppermute | solution.py:575
  135.8 16.1 %collective-permute-start.33 = (s16[2,1040,128]{2,1,0:T(8,128)(2,1)}, s16[2,1040,128]{2,1,0:T(8,128)(2,1)}, u32[]{:S(2)}, u32[]{:S(2)}) collective-permute-start(s16[2,1040,128]{2,1,0:T(8,128)(2,1)} %get-tuple-element.53), channel_id=1, source_target_pairs={{1,0},{2,1},{3,2},{5,4},{6,5},{7,6},{9,8},{10,9},{11,10},{13,12},{... | collective-permute-start | bytes 1597448 | tf_op jit(solution)/shard_map/ppermute | solution.py:575
  137.1 16.1 %collective-permute-start.35 = (s16[2,1040,128]{2,1,0:T(8,128)(2,1)}, s16[2,1040,128]{2,1,0:T(8,128)(2,1)S(1)}, u32[]{:S(2)}, u32[]{:S(2)}) collective-permute-start(s16[2,1040,128]{2,1,0:T(8,128)(2,1)} %get-tuple-element.53), channel_id=1, source_target_pairs={{4,0},{8,4},{12,8},{16,12},{20,16},{24,20},{28,24},{5,1},{9,5},{13... | collective-permute-start | bytes 1597448 | tf_op jit(solution)/shard_map/ppermute | solution.py:575
  138.4 30.5 %collective-permute-start.34 = (s16[2,1040,128]{2,1,0:T(8,128)(2,1)}, s16[2,1040,128]{2,1,0:T(8,128)(2,1)S(1)}, u32[]{:S(2)}, u32[]{:S(2)}) collective-permute-start(s16[2,1040,128]{2,1,0:T(8,128)(2,1)} %get-tuple-element.53), channel_id=1, source_target_pairs={{0,4},{4,8},{8,12},{12,16},{16,20},{20,24},{24,28},{1,5},{5,9},{9,... | collective-permute-start | bytes 1597448 | tf_op jit(solution)/shard_map/ppermute | solution.py:575
  147.0 21.9 %collective-permute-start.36 = (s16[2,1040,128]{2,1,0:T(8,128)(2,1)}, s16[2,1040,128]{2,1,0:T(8,128)(2,1)S(1)}, u32[]{:S(2)}, u32[]{:S(2)}) collective-permute-start(s16[2,1040,128]{2,1,0:T(8,128)(2,1)} %collective-permute-done.32.near), channel_id=1, source_target_pairs={{0,4},{4,8},{8,12},{12,16},{16,20},{20,24},{24,28},{1,5},{5,9},{9,... | collective-permute-start | bytes 1597448 | tf_op jit(solution)/shard_map/ppermute | solution.py:575
  151.9 17.0 %collective-permute-start.37 = (s16[2,1040,128]{2,1,0:T(8,128)(2,1)}, s16[2,1040,128]{2,1,0:T(8,128)(2,1)S(1)}, u32[]{:S(2)}, u32[]{:S(2)}) collective-permute-start(s16[2,1040,128]{2,1,0:T(8,128)(2,1)} %collective-permute-done.33.far), channel_id=1, source_target_pairs={{0,4},{4,8},{8,12},{12,16},{16,20},{20,24},{24,28},{1,5},{5,9},{9,... | collective-permute-start | bytes 1597448 | tf_op jit(solution)/shard_map/ppermute | solution.py:575
  153.2 16.5 %collective-permute-start.38 = (s16[2,1040,128]{2,1,0:T(8,128)(2,1)S(1)}, s16[2,1040,128]{2,1,0:T(8,128)(2,1)}, u32[]{:S(2)}, u32[]{:S(2)}) collective-permute-start(s16[2,1040,128]{2,1,0:T(8,128)(2,1)S(1)} %collective-permute-done.35.refs_2_), channel_id=1, source_target_pairs={{0,1},{1,2},{2,3},{4,5},{5,6},{6,7},{8,9},{9,10},{10,11},{12,13},{... | collective-permute-start | bytes 1597448 | tf_op jit(solution)/shard_map/ppermute | solution.py:575
  158.1 16.7 %collective-permute-start.39 = (s16[2,1040,128]{2,1,0:T(8,128)(2,1)S(1)}, s16[2,1040,128]{2,1,0:T(8,128)(2,1)}, u32[]{:S(2)}, u32[]{:S(2)}) collective-permute-start(s16[2,1040,128]{2,1,0:T(8,128)(2,1)S(1)} %collective-permute-done.35.refs_2_), channel_id=1, source_target_pairs={{1,0},{2,1},{3,2},{5,4},{6,5},{7,6},{9,8},{10,9},{11,10},{13,12},{... | collective-permute-start | bytes 1597448 | tf_op jit(solution)/shard_map/ppermute | solution.py:575
  (34 other events, 404.9 us)
where the time goes:
time: 204 us; the launch traced here: 203 us
  waiting for transfers between devices  74.1 us (36%)
  starting transfers between devices  55.3 us (27%)
  Pallas kernels  52.3 us (26%)
  local copies, waits for them, and re-layouts  14.7 us (7%)
  other arithmetic  5.29 us (3%)
    ppermute x16, waiting for transfers between devices, shared_ratio(): total = total + lax.ppermute(total, 'wide', partner_of(count, bit))  41.9 us
    ppermute x16, starting transfers between devices, shared_ratio(): total = total + lax.ppermute(total, 'wide', partner_of(count, bit))  28.3 us
    pallas_call x1, Pallas kernels, window_correlations(): pl.pallas_call(functools.partial(window_body, count), out_shape=jax.Shape...  24 us
    pallas_call x9, Pallas kernels, sweep_step(): pl.pallas_call(functools.partial(sweep_body, back, forward), grid=(1,), i...  21.7 us
    ppermute x8, starting transfers between devices, shifted(): return lax.ppermute(value, axis, pairs)  18.9 us
    ppermute x8, waiting for transfers between devices, shifted(): return lax.ppermute(value, axis, pairs)  14.8 us
    ppermute x8, waiting for transfers between devices, shared_ratio(): return (ratio, lax.ppermute(ratio, 'wide', pair))  8.74 us
    ppermute x8, waiting for transfers between devices, shared_ratio(): total = kept + lax.ppermute(sent, 'wide', pair)  8.64 us
  transfers between devices with their start and end apart: 41, of which 36 were waited for; matrix products, arithmetic and copies ran while one was open for 4% of the time, Pallas kernels for 4%

commit v1 on v0

--- a/solution.py
+++ b/solution.py
@@ -15,8 +15,6 @@
 MIDDLE = 32768.0
 GRAIN = 16.0
 SPARE = 16
-STEPS = 1
-UNROLL = False
 LIMIT = 24 * 1024 * 1024
 WIDE_LIMIT = 32 * 1024 * 1024
 GROUPS = 2
@@ -398,139 +396,125 @@
     return jnp.concatenate(parts, axis=1)[:, :count]
 
 
-def sweep_body(back, forward, parity_ref, *refs):
+def updated(volume, ratio, tile, member, weights_ref):
+    placement = placed_tiles(tile, ratio.shape[0])
+    spread = mul(placement, ratio).astype(jnp.bfloat16)
+    return volume * jnp.exp(chosen_products(spread, member, weights_ref))
+
+
+def sweep_body(back, forward, volume_ref, *refs):
     refs = list(refs)
-    volume_ref = refs.pop(0)
     if back:
-        own_ratio, other_ratio, back_tile, back_member, back_weights = refs[:5]
-        refs = refs[5:]
+        ratio_ref, back_tile, back_member, back_weights = refs[:4]
+        refs = refs[4:]
     if forward:
         next_row, next_member, next_weights = refs[:3]
         refs = refs[3:]
+    volume = volume_ref[...]
     if back:
-        volume_out = refs.pop(0)
-    exposures, columns, depth = volume_ref.shape
-    block = columns // STEPS
-    odd = parity_ref[0] == 1
-    if back:
-        own, other = own_ratio[...], other_ratio[...]
-        ratios = [jnp.where(odd, other, own), jnp.where(odd, own, other)]
-        ratios = jnp.concatenate(ratios, axis=1)
-    tiles = refs[0].shape[0]
-
-    def one_block(i, total):
-        place = pl.ds(pl.multiple_of(i * block, block), block)
-        volume = volume_ref[:, place, :].reshape(exposures * block, depth)
-        if back:
-            placement = placed_tiles(back_tile[0, place, :], own.shape[0])
-            spread = mul(placement, ratios).astype(jnp.bfloat16)
-            spread = jnp.concatenate(
-                [spread[:, e * LANES : (e + 1) * LANES] for e in range(exposures)], axis=0
-            )
-            member = back_member[0, place, :]
-            volume = volume * jnp.exp(chosen_products(spread, member, back_weights))
-            volume_out[:, place, :] = volume.reshape(exposures, block, depth)
-        if forward:
-            member = next_member[0, place, :]
-            projected = chosen_products(volume.astype(jnp.bfloat16), member, next_weights)
-            parts = list(halves(projected))
-            parts = [p[e * block : (e + 1) * block] for p in parts for e in range(exposures)]
-            rows = lax.broadcasted_iota(jnp.int32, (tiles, block), 0)
-            hit = next_row[0, pl.ds(i, 1), :] == rows
-            placement = jnp.where(hit, 1.0, 0.0).astype(jnp.bfloat16)
-            value = mul(placement, jnp.concatenate(parts, axis=1))
-            size = value.shape[1] // 2
-            total = total + (value[:, :size] + value[:, size:])
-        return total
-
+        volume = updated(volume, ratio_ref[...], back_tile[0], back_member[0], back_weights)
+        refs.pop(0)[...] = volume
     if forward:
-        start = jnp.zeros((tiles, exposures * depth), jnp.float32)
-        if UNROLL:
-            for i in range(STEPS):
-                start = one_block(i, start)
-            total = start
-        else:
-            total = lax.fori_loop(0, STEPS, one_block, start)
-        kept_ref, sent_ref = refs
-        first, second = total[:, :depth], total[:, depth:]
-        kept_ref[...] = jnp.where(odd, second, first)
-        sent_ref[...] = jnp.where(odd, first, second)
-    else:
-        lax.fori_loop(0, STEPS, one_block, 0)
-        (code_ref,) = refs
-        for e in range(exposures):
-            logs = jnp.log(jnp.maximum(volume_out[e], 1e-37))
-            least = jnp.floor(jnp.min(logs, axis=0, keepdims=True) * GRAIN)
-            width = jnp.floor(jnp.max(logs, axis=0, keepdims=True) * GRAIN - least) + 1.0
-            rate = (GRAIN * LEVELS) / width
-            level = jnp.floor((logs - least / GRAIN) * rate + 0.5) - MIDDLE
-            code_ref[e, :columns, :] = level.astype(jnp.int32).astype(jnp.int16)
-            row = lax.broadcasted_iota(jnp.int32, (SPARE, depth), 0)
-            extra = jnp.where(row == 0, least, jnp.where(row == 1, width, 0.0))
-            code_ref[e, columns:, :] = extra.astype(jnp.int32).astype(jnp.int16)
-
-
-def sweep_step(parity, volume, ratios, columns, weights, weights_turned, tiles, camera, following):
-    exposures, count, depth = volume.shape
-    pixels = weights.shape[2]
+        (partial_ref,) = refs
+        tiles = partial_ref.shape[0]
+        projected = chosen_products(volume.astype(jnp.bfloat16), next_member[0], next_weights)
+        rows = lax.broadcasted_iota(jnp.int32, (tiles, volume.shape[0]), 0)
+        placement = jnp.where(next_row[0] == rows, 1.0, 0.0).astype(jnp.bfloat16)
+        value = mul(placement, jnp.concatenate(halves(projected), axis=1))
+        size = value.shape[1] // 2
+        partial_ref[...] = value[:, :size] + value[:, size:]
+
+
+def last_body(parity_ref, *refs):
+    kept, other, own_ratio, other_ratio, tile, member, weights, volume_out, code_out = refs
+    columns, depth = kept.shape
+    parity = parity_ref[0]
+    pairs = ((parity, kept, own_ratio), (1 - parity, other, other_ratio))
+    for e, volume_ref, ratio_ref in pairs:
+        volume = updated(volume_ref[...], ratio_ref[...], tile[0], member[0], weights)
+        volume_out[e] = volume
+        logs = jnp.log(jnp.maximum(volume, 1e-37))
+        least = jnp.floor(jnp.min(logs, axis=0, keepdims=True) * GRAIN)
+        width = jnp.floor(jnp.max(logs, axis=0, keepdims=True) * GRAIN - least) + 1.0
+        rate = (GRAIN * LEVELS) / width
+        level = jnp.floor((logs - least / GRAIN) * rate + 0.5) - MIDDLE
+        code_out[e, :columns, :] = level.astype(jnp.int32).astype(jnp.int16)
+        row = lax.broadcasted_iota(jnp.int32, (SPARE, depth), 0)
+        extra = jnp.where(row == 0, least, jnp.where(row == 1, width, 0.0))
+        code_out[e, columns:, :] = extra.astype(jnp.int32).astype(jnp.int16)
+
+
+def taken(value, index):
+    shape = (1,) + value.shape[1:]
+    return pl.BlockSpec(shape, lambda i: (index,) + (0,) * (len(shape) - 1))
+
+
+def whole(value):
+    return pl.BlockSpec(value.shape, lambda i: (0,) * len(value.shape))
+
+
+def sweep_step(volume, ratio, columns, weights, weights_turned, tiles, camera, following):
     back, forward = camera is not None, following is not None
     rows, tile_values, members = columns
-
-    def taken(value, index):
-        shape = (1,) + value.shape[1:]
-        return pl.BlockSpec(shape, lambda i: (index,) + (0,) * (len(shape) - 1))
-
-    def whole(shape):
-        return pl.BlockSpec(shape, lambda i: (0,) * len(shape))
-
-    operands = [parity, volume]
-    specs = [pl.BlockSpec(memory_space=pltpu.SMEM), whole(volume.shape)]
-    shapes = []
+    operands, specs, shapes = [volume], [whole(volume)], []
     if back:
-        operands += [*ratios, tile_values, members, weights]
-        specs += [whole((tiles, pixels))] * 2
-        specs += [taken(tile_values, camera), taken(members, camera), taken(weights, camera)]
+        operands += [ratio, tile_values, members, weights]
+        specs += [whole(ratio)] + [taken(value, camera) for value in operands[-3:]]
         shapes.append(jax.ShapeDtypeStruct(volume.shape, jnp.float32))
     if forward:
         operands += [rows, members, weights_turned]
         specs += [taken(value, following) for value in operands[-3:]]
-        shapes += [jax.ShapeDtypeStruct((tiles, pixels), jnp.float32)] * 2
-    else:
-        shapes.append(jax.ShapeDtypeStruct((exposures, count + SPARE, depth), jnp.int16))
-    result = pl.pallas_call(
+        shapes.append(jax.ShapeDtypeStruct((tiles, weights.shape[2]), jnp.float32))
+    return pl.pallas_call(
         functools.partial(sweep_body, back, forward),
         grid=(1,),
         in_specs=specs,
-        out_specs=[whole(value.shape) for value in shapes],
+        out_specs=[whole(value) for value in shapes],
         out_shape=shapes,
         compiler_params=pltpu.CompilerParams(vmem_limit_bytes=LIMIT),
         name="sweep",
     )(*operands)
-    return (result[0] if back else volume), (result[-2:] if forward else result[-1])
+
+
+def last_step(parity, volumes, ratios, columns, weights, camera):
+    count, depth = volumes[0].shape
+    exposures = len(volumes)
+    tables = [columns[1], columns[2], weights]
+    shapes = [
+        jax.ShapeDtypeStruct((exposures, count, depth), jnp.float32),
+        jax.ShapeDtypeStruct((exposures, count + SPARE, depth), jnp.int16),
+    ]
+    return pl.pallas_call(
+        last_body,
+        grid=(1,),
+        in_specs=[pl.BlockSpec(memory_space=pltpu.SMEM)]
+        + [whole(value) for value in (*volumes, *ratios)]
+        + [taken(value, camera) for value in tables],
+        out_specs=[whole(value) for value in shapes],
+        out_shape=shapes,
+        compiler_params=pltpu.CompilerParams(vmem_limit_bytes=LIMIT),
+        name="last",
+    )(parity, *volumes, *ratios, *tables)
 
 
 def column_tables(target, member):
     shape = target.shape + (LANES,)
     tile_values = jnp.broadcast_to(target.astype(jnp.bfloat16)[..., None], shape)
     members = jnp.broadcast_to(member.astype(jnp.bfloat16)[..., None], shape)
-    rows = target.reshape(target.shape[0], STEPS, target.shape[1] // STEPS)
-    return rows, tile_values, members
+    return target[:, None, :], tile_values, members
 
 
 def partner_of(count, bit):
     return [(i, i ^ bit) for i in range(count)]
 
 
-def shared_ratio(kept, sent, picture):
+def shared_ratio(total, picture):
     count = lax.axis_size("wide")
-    pair = partner_of(count, 1)
-    total = kept + lax.ppermute(sent, "wide", pair)
     bit = 2
     while bit < count:
         total = total + lax.ppermute(total, "wide", partner_of(count, bit))
         bit *= 2
-    ratio = (picture - jnp.log(total + 1.0)).astype(jnp.bfloat16)
-    return ratio, lax.ppermute(ratio, "wide", pair)
+    return (picture - jnp.log(total + 1.0)).astype(jnp.bfloat16)
 
 
 def reconstructed(initial, images, blocks, lib_index, tile_map):
@@ -548,7 +532,7 @@
     tables = column_tables(
         target.reshape(cameras, columns), lib_index.reshape(cameras, columns)
     )
-    parity = (own_index % 2).reshape(1)
+    parity = own_index % 2
     pictures = jnp.log(images.reshape(exposures, cameras, tile_count, pixels) + 1.0)
     by_core = jnp.broadcast_to(pictures[None], (count // 2,) + pictures.shape)
     by_core = by_core.reshape((count, cameras, tile_count, pixels))
@@ -556,16 +540,28 @@
     gathered = gathered.transpose(1, 0, 2, 3).reshape(cameras, tiles, pixels)
     turned = blocks.transpose(0, 1, 3, 2)
     volume = initial.reshape(exposures, columns, depth)
+    kept = lax.dynamic_index_in_dim(volume, parity, 0, keepdims=False)
+    other = lax.dynamic_index_in_dim(volume, 1 - parity, 0, keepdims=False)
     order = [camera for _ in range(SWEEPS) for camera in range(cameras)]
     step = functools.partial(
         sweep_step, columns=tables, weights=blocks, weights_turned=turned, tiles=tiles
     )
-    volume, partial_value = step(parity, volume, None, camera=None, following=order[0])
-    for place, camera in enumerate(order):
-        following = order[place + 1] if place + 1 < len(order) else None
-        ratios = shared_ratio(*partial_value, gathered[camera])
-        volume, partial_value = step(parity, volume, ratios, camera=camera, following=following)
-    return volume, partial_value
+
+    def swapped(value):
+        return lax.ppermute(value, "wide", partner_of(count, 1))
+
+    (sent,) = step(other, None, camera=None, following=order[0])
+    (own,) = step(kept, None, camera=None, following=order[0])
+    for camera, following in zip(order, order[1:]):
+        ratio = shared_ratio(own + swapped(sent), gathered[camera])
+        other_ratio = swapped(ratio)
+        (kept,) = step(kept, ratio, camera=camera, following=None)
+        other, sent = step(other, other_ratio, camera=camera, following=following)
+        (own,) = step(kept, None, camera=None, following=following)
+    ratio = shared_ratio(own + swapped(sent), gathered[order[-1]])
+    return last_step(
+        parity.reshape(1), (kept, other), (ratio, swapped(ratio)), tables, blocks, order[-1]
+    )
 
 
 def neighbours(own):

time: 204 us -> 199 us (0.975)
  waiting for transfers between devices: 74.1 us -> 68.5 us
  Pallas kernels: 52.3 us -> 55.5 us
    ppermute x16, waiting for transfers between devices: 17.4 us -> 8.97 us  [swapped(): return lax.ppermute(value, 'wide', partner_of(count, 1))]
    pallas_call x0 -> x1, Pallas kernels: none -> 2.86 us  [last_step(): pl.pallas_call(last_body, grid=(1,), in_specs=[pl.BlockSpec(memory_space=...]
    unnamed x35 -> x43, local copies, waits for them, and re-layouts: 7.75 us -> 5.85 us
    pallas_call x9 -> x23, Pallas kernels: 21.7 us -> 22.1 us  [sweep_step(): pl.pallas_call(functools.partial(sweep_body, back, forward), grid=(1,), i...]
  transfers between devices with their start and end apart: 41 -> 41, of which waited for: 36 -> 29; matrix products, arithmetic and copies ran while one was open for 4% -> 4% of each run, Pallas kernels for 4% -> 9%
where the time goes in v1:
time: 199 us; the launch traced here: 198 us
  waiting for transfers between devices  68.5 us (34%)
  Pallas kernels  55.5 us (28%)
  starting transfers between devices  54.8 us (28%)
  local copies, waits for them, and re-layouts  12.8 us (6%)
  other arithmetic  5.29 us (3%)
    ppermute x16, waiting for transfers between devices, shared_ratio(): total = total + lax.ppermute(total, 'wide', partner_of(count, bit))  43 us
    ppermute x16, starting transfers between devices, shared_ratio(): total = total + lax.ppermute(total, 'wide', partner_of(count, bit))  28.4 us
    pallas_call x1, Pallas kernels, window_correlations(): pl.pallas_call(functools.partial(window_body, count), out_shape=jax.Shape...  24 us
    pallas_call x23, Pallas kernels, sweep_step(): pl.pallas_call(functools.partial(sweep_body, back, forward), grid=(1,), i...  22.1 us
    ppermute x8, starting transfers between devices, shifted(): return lax.ppermute(value, axis, pairs)  18.5 us
    ppermute x8, waiting for transfers between devices, shifted(): return lax.ppermute(value, axis, pairs)  16.5 us
    ppermute x16, waiting for transfers between devices, swapped(): return lax.ppermute(value, 'wide', partner_of(count, 1))  8.97 us
    pallas_call x1, Pallas kernels, middle_spectra(): pl.pallas_call(functools.partial(middle_body, count), out_shape=[jax.Shap...  6.62 us
  transfers between devices with their start and end apart: 41, of which 29 were waited for; matrix products, arithmetic and copies ran while one was open for 4% of the time, Pallas kernels for 9%

profile of v1, /device:TPU:0, one launch (start us, length us, event | category | flops | bytes accessed | tf_op | source)
XLA Modules:
  0.0 198.3 jit_solution(5379073556006823071)
XLA Ops:
  2.3 5.2 %all-to-all-start = ((f32[8,4,18,128]{3,1,2,0:T(4,128)}), f32[8,4,18,128]{3,1,2,0:T(4,128)S(1)}, u32[]{:S(2)}, u32[]{:S(2)}) async-start(f32[8,4,18,128]{3,1,2,0:T(4,128)} %bitcast.4), calls=%async_computation | async-start | bytes 589824 | tf_op jit(solution)/shard_map/all_to_all | solution.py:539
  17.8 2.7 %collective-permute-done.1 = f32[144,128]{1,0:T(8,128)S(1)} collective-permute-done((f32[144,128]{1,0:T(8,128)S(1)}, f32[144,128]{1,0:T(8,128)S(1)}, u32[]{:S(2)}, u32[]{:S(2)}) %collective-permute-start.1) | collective-permute-done | bytes 73760 | tf_op jit(solution)/shard_map/ppermute | solution.py:515
  34.6 2.8 %collective-permute-done.5 = f32[144,128]{1,0:T(8,128)S(1)} collective-permute-done((f32[144,128]{1,0:T(8,128)S(1)}, f32[144,128]{1,0:T(8,128)S(1)}, u32[]{:S(2)}, u32[]{:S(2)}) %collective-permute-start.5) | collective-permute-done | bytes 73760 | tf_op jit(solution)/shard_map/ppermute | solution.py:515
  39.2 2.7 %collective-permute-done.6 = f32[144,128]{1,0:T(8,128)S(1)} collective-permute-done((f32[144,128]{1,0:T(8,128)S(1)}, f32[144,128]{1,0:T(8,128)S(1)}, u32[]{:S(2)}, u32[]{:S(2)}) %collective-permute-start.6) | collective-permute-done | bytes 73760 | tf_op jit(solution)/shard_map/ppermute | solution.py:515
  48.2 2.8 %collective-permute-done.9 = f32[144,128]{1,0:T(8,128)S(1)} collective-permute-done((f32[144,128]{1,0:T(8,128)S(1)}, f32[144,128]{1,0:T(8,128)S(1)}, u32[]{:S(2)}, u32[]{:S(2)}) %collective-permute-start.9) | collective-permute-done | bytes 73760 | tf_op jit(solution)/shard_map/ppermute | solution.py:515
  52.8 2.6 %collective-permute-done.10 = f32[144,128]{1,0:T(8,128)S(1)} collective-permute-done((f32[144,128]{1,0:T(8,128)S(1)}, f32[144,128]{1,0:T(8,128)S(1)}, u32[]{:S(2)}, u32[]{:S(2)}) %collective-permute-start.10) | collective-permute-done | bytes 73760 | tf_op jit(solution)/shard_map/ppermute | solution.py:515
  61.7 2.8 %collective-permute-done.13 = f32[144,128]{1,0:T(8,128)S(1)} collective-permute-done((f32[144,128]{1,0:T(8,128)S(1)}, f32[144,128]{1,0:T(8,128)S(1)}, u32[]{:S(2)}, u32[]{:S(2)}) %collective-permute-start.13) | collective-permute-done | bytes 73760 | tf_op jit(solution)/shard_map/ppermute | solution.py:515
  66.3 2.6 %collective-permute-done.14 = f32[144,128]{1,0:T(8,128)S(1)} collective-permute-done((f32[144,128]{1,0:T(8,128)S(1)}, f32[144,128]{1,0:T(8,128)S(1)}, u32[]{:S(2)}, u32[]{:S(2)}) %collective-permute-start.14) | collective-permute-done | bytes 73760 | tf_op jit(solution)/shard_map/ppermute | solution.py:515
  75.4 2.8 %collective-permute-done.17 = f32[144,128]{1,0:T(8,128)S(1)} collective-permute-done((f32[144,128]{1,0:T(8,128)S(1)}, f32[144,128]{1,0:T(8,128)S(1)}, u32[]{:S(2)}, u32[]{:S(2)}) %collective-permute-start.17) | collective-permute-done | bytes 73760 | tf_op jit(solution)/shard_map/ppermute | solution.py:515
  80.0 2.6 %collective-permute-done.18 = f32[144,128]{1,0:T(8,128)S(1)} collective-permute-done((f32[144,128]{1,0:T(8,128)S(1)}, f32[144,128]{1,0:T(8,128)S(1)}, u32[]{:S(2)}, u32[]{:S(2)}) %collective-permute-start.18) | collective-permute-done | bytes 73760 | tf_op jit(solution)/shard_map/ppermute | solution.py:515
  89.0 2.8 %collective-permute-done.21 = f32[144,128]{1,0:T(8,128)S(1)} collective-permute-done((f32[144,128]{1,0:T(8,128)S(1)}, f32[144,128]{1,0:T(8,128)S(1)}, u32[]{:S(2)}, u32[]{:S(2)}) %collective-permute-start.21) | collective-permute-done | bytes 73760 | tf_op jit(solution)/shard_map/ppermute | solution.py:515
  93.6 2.6 %collective-permute-done.22 = f32[144,128]{1,0:T(8,128)S(1)} collective-permute-done((f32[144,128]{1,0:T(8,128)S(1)}, f32[144,128]{1,0:T(8,128)S(1)}, u32[]{:S(2)}, u32[]{:S(2)}) %collective-permute-start.22) | collective-permute-done | bytes 73760 | tf_op jit(solution)/shard_map/ppermute | solution.py:515
  102.5 2.8 %collective-permute-done.25 = f32[144,128]{1,0:T(8,128)S(1)} collective-permute-done((f32[144,128]{1,0:T(8,128)S(1)}, f32[144,128]{1,0:T(8,128)S(1)}, u32[]{:S(2)}, u32[]{:S(2)}) %collective-permute-start.25) | collective-permute-done | bytes 73760 | tf_op jit(solution)/shard_map/ppermute | solution.py:515
  107.1 2.6 %collective-permute-done.26 = f32[144,128]{1,0:T(8,128)S(1)} collective-permute-done((f32[144,128]{1,0:T(8,128)S(1)}, f32[144,128]{1,0:T(8,128)S(1)}, u32[]{:S(2)}, u32[]{:S(2)}) %collective-permute-start.26) | collective-permute-done | bytes 73760 | tf_op jit(solution)/shard_map/ppermute | solution.py:515
  116.2 2.8 %collective-permute-done.29 = f32[144,128]{1,0:T(8,128)S(1)} collective-permute-done((f32[144,128]{1,0:T(8,128)S(1)}, f32[144,128]{1,0:T(8,128)S(1)}, u32[]{:S(2)}, u32[]{:S(2)}) %collective-permute-start.29) | collective-permute-done | bytes 73760 | tf_op jit(solution)/shard_map/ppermute | solution.py:515
  124.7 2.9 %last.1 = (f32[2,1024,128]{2,1,0:T(8,128)}, s16[2,1040,128]{2,1,0:T(8,128)(2,1)}) custom-call(s32[1]{0:T(128)} %bitcast.parity_ref, f32[1024,128]{1,0:T(8,128)S(1)} %sweep.43.volume_ref.refs_0_, f32[1024,128]{1,0:T(8,128)S(1)} %get-tuple-element.32.refs_1_, bf16[144,128]{1,0:T(8,128)(2,1)S(1)} %subtract_convert_fusion.refs_2_, ...), custom_call_target="tpu_custom_call" | custom-call | tf_op jit(solution)/shard_map/last/pallas_call | solution.py:487
  127.6 4.3 %collective-permute-start.32 = (s16[2,1040,128]{2,1,0:T(8,128)(2,1)}, s16[2,1040,128]{2,1,0:T(8,128)(2,1)}, u32[]{:S(2)}, u32[]{:S(2)}) collective-permute-start(s16[2,1040,128]{2,1,0:T(8,128)(2,1)} %get-tuple-element.35), channel_id=1, source_target_pairs={{0,1},{1,2},{2,3},{4,5},{5,6},{6,7},{8,9},{9,10},{10,11},{12,13},{... | collective-permute-start | bytes 1597448 | tf_op jit(solution)/shard_map/ppermute | solution.py:571
  134.4 3.1 %collective-permute-start.34 = (s16[2,1040,128]{2,1,0:T(8,128)(2,1)}, s16[2,1040,128]{2,1,0:T(8,128)(2,1)S(1)}, u32[]{:S(2)}, u32[]{:S(2)}) collective-permute-start(s16[2,1040,128]{2,1,0:T(8,128)(2,1)} %get-tuple-element.35), channel_id=1, source_target_pairs={{0,4},{4,8},{8,12},{12,16},{16,20},{20,24},{24,28},{1,5},{5,9},{9,... | collective-permute-start | bytes 1597448 | tf_op jit(solution)/shard_map/ppermute | solution.py:571
  137.5 5.5 %collective-permute-done.32.near = s16[2,1040,128]{2,1,0:T(8,128)(2,1)} collective-permute-done((s16[2,1040,128]{2,1,0:T(8,128)(2,1)}, s16[2,1040,128]{2,1,0:T(8,128)(2,1)}, u32[]{:S(2)}, u32[]{:S(2)}) %collective-permute-start.32) | collective-permute-done | bytes 532512 | tf_op jit(solution)/shard_map/ppermute | solution.py:571
  144.4 3.6 %collective-permute-done.33.far = s16[2,1040,128]{2,1,0:T(8,128)(2,1)} collective-permute-done((s16[2,1040,128]{2,1,0:T(8,128)(2,1)}, s16[2,1040,128]{2,1,0:T(8,128)(2,1)}, u32[]{:S(2)}, u32[]{:S(2)}) %collective-permute-start.33) | collective-permute-done | bytes 532512 | tf_op jit(solution)/shard_map/ppermute | solution.py:571
  149.3 4.7 %collective-permute-start.38 = (s16[2,1040,128]{2,1,0:T(8,128)(2,1)S(1)}, s16[2,1040,128]{2,1,0:T(8,128)(2,1)}, u32[]{:S(2)}, u32[]{:S(2)}) collective-permute-start(s16[2,1040,128]{2,1,0:T(8,128)(2,1)S(1)} %collective-permute-done.35.refs_2_), channel_id=1, source_target_pairs={{0,1},{1,2},{2,3},{4,5},{5,6},{6,7},{8,9},{9,10},{10,11},{12,13},{... | collective-permute-start | bytes 1597448 | tf_op jit(solution)/shard_map/ppermute | solution.py:571
  156.8 6.6 %middle.1 = (f32[4,72,32,128]{3,2,1,0:T(8,128)S(1)}, f32[4,8,128]{2,1,0:T(8,128)S(1)}) custom-call(s32[4,3]{1,0:T(4,128)S(1)} %pad_add_fusion.starts, f32[2,1024,128]{2,1,0:T(8,128)S(1)} %copy-done.5, s16[2,1040,128]{2,1,0:T(8,128)(2,1)} %collective-permute-done.32.near, s16[2,1040,128]{2,1,0:T(8,128)(2,1)} %collective-permute-done.33.far, ...), custom_call_target="tpu_custom_call" | custom-call | tf_op jit(solution)/shard_map/middle/pallas_call | solution.py:313
  165.3 5.6 %collective-permute-done.39.refs_6_ = s16[2,1040,128]{2,1,0:T(8,128)(2,1)} collective-permute-done((s16[2,1040,128]{2,1,0:T(8,128)(2,1)S(1)}, s16[2,1040,128]{2,1,0:T(8,128)(2,1)}, u32[]{:S(2)}, u32[]{:S(2)}) %collective-permute-start.39) | collective-permute-done | bytes 532512 | tf_op jit(solution)/shard_map/ppermute | solution.py:571
  172.8 24.0 %windows.1 = f32[16,2048]{1,0:T(8,128)S(1)} custom-call(s32[4,3]{1,0:T(4,128)S(1)} %pad_add_fusion.starts, f32[4,8,128]{2,1,0:T(8,128)S(1)} %get-tuple-element.36.stats, f32[4,72,32,128]{3,2,1,0:T(8,128)S(1)} %get-tuple-element.37.refs_0_, s16[2,1040,128]{2,1,0:T(8,128)(2,1)S(1)} %collective-permute-done.34.refs_1_, ...), custom_call_target="tpu_custom_call" | custom-call | tf_op jit(solution)/shard_map/windows/pallas_call | solution.py:341
  (170 shorter events, 93.3 us)
Async XLA Ops:
  2.3 20.4 %all-to-all-start = ((f32[8,4,18,128]{3,1,2,0:T(4,128)}), f32[8,4,18,128]{3,1,2,0:T(4,128)S(1)}, u32[]{:S(2)}, u32[]{:S(2)}) async-start(f32[8,4,18,128]{3,1,2,0:T(4,128)} %bitcast.4), calls=%async_computation | async-start | bytes 589824 | tf_op jit(solution)/shard_map/all_to_all | solution.py:539
  15.8 4.6 %collective-permute-start.1 = (f32[144,128]{1,0:T(8,128)S(1)}, f32[144,128]{1,0:T(8,128)S(1)}, u32[]{:S(2)}, u32[]{:S(2)}) collective-permute-start(f32[144,128]{1,0:T(8,128)S(1)} %add.145), channel_id=1, source_target_pairs={{0,8},{4,12},{8,0},{12,4},{16,24},{20,28},{24,16},{28,20},{1,9},{5... | collective-permute-start | bytes 221192 | tf_op jit(solution)/shard_map/ppermute | solution.py:515
  21.1 4.7 %collective-permute-start.2 = (f32[144,128]{1,0:T(8,128)}, f32[144,128]{1,0:T(8,128)}, u32[]{:S(2)}, u32[]{:S(2)}) collective-permute-start(f32[144,128]{1,0:T(8,128)} %add.146), channel_id=1, source_target_pairs={{0,16},{4,20},{8,24},{12,28},{16,0},{20,4},{24,8},{28,12},{1,17},{... | collective-permute-start | bytes 221192 | tf_op jit(solution)/shard_map/ppermute | solution.py:515
  32.9 4.6 %collective-permute-start.5 = (f32[144,128]{1,0:T(8,128)S(1)}, f32[144,128]{1,0:T(8,128)S(1)}, u32[]{:S(2)}, u32[]{:S(2)}) collective-permute-start(f32[144,128]{1,0:T(8,128)S(1)} %add.149), channel_id=1, source_target_pairs={{0,8},{4,12},{8,0},{12,4},{16,24},{20,28},{24,16},{28,20},{1,9},{5... | collective-permute-start | bytes 221192 | tf_op jit(solution)/shard_map/ppermute | solution.py:515
  37.4 4.4 %collective-permute-start.6 = (f32[144,128]{1,0:T(8,128)S(1)}, f32[144,128]{1,0:T(8,128)S(1)}, u32[]{:S(2)}, u32[]{:S(2)}) collective-permute-start(f32[144,128]{1,0:T(8,128)S(1)} %add.150), channel_id=1, source_target_pairs={{0,16},{4,20},{8,24},{12,28},{16,0},{20,4},{24,8},{28,12},{1,17},{... | collective-permute-start | bytes 221192 | tf_op jit(solution)/shard_map/ppermute | solution.py:515
  46.4 4.6 %collective-permute-start.9 = (f32[144,128]{1,0:T(8,128)S(1)}, f32[144,128]{1,0:T(8,128)S(1)}, u32[]{:S(2)}, u32[]{:S(2)}) collective-permute-start(f32[144,128]{1,0:T(8,128)S(1)} %add.153), channel_id=1, source_target_pairs={{0,8},{4,12},{8,0},{12,4},{16,24},{20,28},{24,16},{28,20},{1,9},{5... | collective-permute-start | bytes 221192 | tf_op jit(solution)/shard_map/ppermute | solution.py:515
  51.0 4.4 %collective-permute-start.10 = (f32[144,128]{1,0:T(8,128)S(1)}, f32[144,128]{1,0:T(8,128)S(1)}, u32[]{:S(2)}, u32[]{:S(2)}) collective-permute-start(f32[144,128]{1,0:T(8,128)S(1)} %add.154), channel_id=1, source_target_pairs={{0,16},{4,20},{8,24},{12,28},{16,0},{20,4},{24,8},{28,12},{1,17},{... | collective-permute-start | bytes 221192 | tf_op jit(solution)/shard_map/ppermute | solution.py:515
  59.9 4.6 %collective-permute-start.13 = (f32[144,128]{1,0:T(8,128)S(1)}, f32[144,128]{1,0:T(8,128)S(1)}, u32[]{:S(2)}, u32[]{:S(2)}) collective-permute-start(f32[144,128]{1,0:T(8,128)S(1)} %add.157), channel_id=1, source_target_pairs={{0,8},{4,12},{8,0},{12,4},{16,24},{20,28},{24,16},{28,20},{1,9},{5... | collective-permute-start | bytes 221192 | tf_op jit(solution)/shard_map/ppermute | solution.py:515
  64.5 4.4 %collective-permute-start.14 = (f32[144,128]{1,0:T(8,128)S(1)}, f32[144,128]{1,0:T(8,128)S(1)}, u32[]{:S(2)}, u32[]{:S(2)}) collective-permute-start(f32[144,128]{1,0:T(8,128)S(1)} %add.158), channel_id=1, source_target_pairs={{0,16},{4,20},{8,24},{12,28},{16,0},{20,4},{24,8},{28,12},{1,17},{... | collective-permute-start | bytes 221192 | tf_op jit(solution)/shard_map/ppermute | solution.py:515
  73.7 4.6 %collective-permute-start.17 = (f32[144,128]{1,0:T(8,128)S(1)}, f32[144,128]{1,0:T(8,128)S(1)}, u32[]{:S(2)}, u32[]{:S(2)}) collective-permute-start(f32[144,128]{1,0:T(8,128)S(1)} %add.161), channel_id=1, source_target_pairs={{0,8},{4,12},{8,0},{12,4},{16,24},{20,28},{24,16},{28,20},{1,9},{5... | collective-permute-start | bytes 221192 | tf_op jit(solution)/shard_map/ppermute | solution.py:515
  78.3 4.4 %collective-permute-start.18 = (f32[144,128]{1,0:T(8,128)S(1)}, f32[144,128]{1,0:T(8,128)S(1)}, u32[]{:S(2)}, u32[]{:S(2)}) collective-permute-start(f32[144,128]{1,0:T(8,128)S(1)} %add.162), channel_id=1, source_target_pairs={{0,16},{4,20},{8,24},{12,28},{16,0},{20,4},{24,8},{28,12},{1,17},{... | collective-permute-start | bytes 221192 | tf_op jit(solution)/shard_map/ppermute | solution.py:515
  87.2 4.6 %collective-permute-start.21 = (f32[144,128]{1,0:T(8,128)S(1)}, f32[144,128]{1,0:T(8,128)S(1)}, u32[]{:S(2)}, u32[]{:S(2)}) collective-permute-start(f32[144,128]{1,0:T(8,128)S(1)} %add.165), channel_id=1, source_target_pairs={{0,8},{4,12},{8,0},{12,4},{16,24},{20,28},{24,16},{28,20},{1,9},{5... | collective-permute-start | bytes 221192 | tf_op jit(solution)/shard_map/ppermute | solution.py:515
  91.8 4.4 %collective-permute-start.22 = (f32[144,128]{1,0:T(8,128)S(1)}, f32[144,128]{1,0:T(8,128)S(1)}, u32[]{:S(2)}, u32[]{:S(2)}) collective-permute-start(f32[144,128]{1,0:T(8,128)S(1)} %add.166), channel_id=1, source_target_pairs={{0,16},{4,20},{8,24},{12,28},{16,0},{20,4},{24,8},{28,12},{1,17},{... | collective-permute-start | bytes 221192 | tf_op jit(solution)/shard_map/ppermute | solution.py:515
  100.7 4.6 %collective-permute-start.25 = (f32[144,128]{1,0:T(8,128)S(1)}, f32[144,128]{1,0:T(8,128)S(1)}, u32[]{:S(2)}, u32[]{:S(2)}) collective-permute-start(f32[144,128]{1,0:T(8,128)S(1)} %add.169), channel_id=1, source_target_pairs={{0,8},{4,12},{8,0},{12,4},{16,24},{20,28},{24,16},{28,20},{1,9},{5... | collective-permute-start | bytes 221192 | tf_op jit(solution)/shard_map/ppermute | solution.py:515
  105.3 4.4 %collective-permute-start.26 = (f32[144,128]{1,0:T(8,128)S(1)}, f32[144,128]{1,0:T(8,128)S(1)}, u32[]{:S(2)}, u32[]{:S(2)}) collective-permute-start(f32[144,128]{1,0:T(8,128)S(1)} %add.170), channel_id=1, source_target_pairs={{0,16},{4,20},{8,24},{12,28},{16,0},{20,4},{24,8},{28,12},{1,17},{... | collective-permute-start | bytes 221192 | tf_op jit(solution)/shard_map/ppermute | solution.py:515
  114.4 4.6 %collective-permute-start.29 = (f32[144,128]{1,0:T(8,128)S(1)}, f32[144,128]{1,0:T(8,128)S(1)}, u32[]{:S(2)}, u32[]{:S(2)}) collective-permute-start(f32[144,128]{1,0:T(8,128)S(1)} %add.173), channel_id=1, source_target_pairs={{0,8},{4,12},{8,0},{12,4},{16,24},{20,28},{24,16},{28,20},{1,9},{5... | collective-permute-start | bytes 221192 | tf_op jit(solution)/shard_map/ppermute | solution.py:515
  127.6 15.5 %collective-permute-start.32 = (s16[2,1040,128]{2,1,0:T(8,128)(2,1)}, s16[2,1040,128]{2,1,0:T(8,128)(2,1)}, u32[]{:S(2)}, u32[]{:S(2)}) collective-permute-start(s16[2,1040,128]{2,1,0:T(8,128)(2,1)} %get-tuple-element.35), channel_id=1, source_target_pairs={{0,1},{1,2},{2,3},{4,5},{5,6},{6,7},{8,9},{9,10},{10,11},{12,13},{... | collective-permute-start | bytes 1597448 | tf_op jit(solution)/shard_map/ppermute | solution.py:571
  131.8 16.1 %collective-permute-start.33 = (s16[2,1040,128]{2,1,0:T(8,128)(2,1)}, s16[2,1040,128]{2,1,0:T(8,128)(2,1)}, u32[]{:S(2)}, u32[]{:S(2)}) collective-permute-start(s16[2,1040,128]{2,1,0:T(8,128)(2,1)} %get-tuple-element.35), channel_id=1, source_target_pairs={{1,0},{2,1},{3,2},{5,4},{6,5},{7,6},{9,8},{10,9},{11,10},{13,12},{... | collective-permute-start | bytes 1597448 | tf_op jit(solution)/shard_map/ppermute | solution.py:571
  133.1 16.1 %collective-permute-start.35 = (s16[2,1040,128]{2,1,0:T(8,128)(2,1)}, s16[2,1040,128]{2,1,0:T(8,128)(2,1)S(1)}, u32[]{:S(2)}, u32[]{:S(2)}) collective-permute-start(s16[2,1040,128]{2,1,0:T(8,128)(2,1)} %get-tuple-element.35), channel_id=1, source_target_pairs={{4,0},{8,4},{12,8},{16,12},{20,16},{24,20},{28,24},{5,1},{9,5},{13... | collective-permute-start | bytes 1597448 | tf_op jit(solution)/shard_map/ppermute | solution.py:571
  134.4 29.0 %collective-permute-start.34 = (s16[2,1040,128]{2,1,0:T(8,128)(2,1)}, s16[2,1040,128]{2,1,0:T(8,128)(2,1)S(1)}, u32[]{:S(2)}, u32[]{:S(2)}) collective-permute-start(s16[2,1040,128]{2,1,0:T(8,128)(2,1)} %get-tuple-element.35), channel_id=1, source_target_pairs={{0,4},{4,8},{8,12},{12,16},{16,20},{20,24},{24,28},{1,5},{5,9},{9,... | collective-permute-start | bytes 1597448 | tf_op jit(solution)/shard_map/ppermute | solution.py:571
  143.0 20.4 %collective-permute-start.36 = (s16[2,1040,128]{2,1,0:T(8,128)(2,1)}, s16[2,1040,128]{2,1,0:T(8,128)(2,1)S(1)}, u32[]{:S(2)}, u32[]{:S(2)}) collective-permute-start(s16[2,1040,128]{2,1,0:T(8,128)(2,1)} %collective-permute-done.32.near), channel_id=1, source_target_pairs={{0,4},{4,8},{8,12},{12,16},{16,20},{20,24},{24,28},{1,5},{5,9},{9,... | collective-permute-start | bytes 1597448 | tf_op jit(solution)/shard_map/ppermute | solution.py:571
  147.9 15.5 %collective-permute-start.37 = (s16[2,1040,128]{2,1,0:T(8,128)(2,1)}, s16[2,1040,128]{2,1,0:T(8,128)(2,1)S(1)}, u32[]{:S(2)}, u32[]{:S(2)}) collective-permute-start(s16[2,1040,128]{2,1,0:T(8,128)(2,1)} %collective-permute-done.33.far), channel_id=1, source_target_pairs={{0,4},{4,8},{8,12},{12,16},{16,20},{20,24},{24,28},{1,5},{5,9},{9,... | collective-permute-start | bytes 1597448 | tf_op jit(solution)/shard_map/ppermute | solution.py:571
  149.3 16.0 %collective-permute-start.38 = (s16[2,1040,128]{2,1,0:T(8,128)(2,1)S(1)}, s16[2,1040,128]{2,1,0:T(8,128)(2,1)}, u32[]{:S(2)}, u32[]{:S(2)}) collective-permute-start(s16[2,1040,128]{2,1,0:T(8,128)(2,1)S(1)} %collective-permute-done.35.refs_2_), channel_id=1, source_target_pairs={{0,1},{1,2},{2,3},{4,5},{5,6},{6,7},{8,9},{9,10},{10,11},{12,13},{... | collective-permute-start | bytes 1597448 | tf_op jit(solution)/shard_map/ppermute | solution.py:571
  153.9 17.0 %collective-permute-start.39 = (s16[2,1040,128]{2,1,0:T(8,128)(2,1)S(1)}, s16[2,1040,128]{2,1,0:T(8,128)(2,1)}, u32[]{:S(2)}, u32[]{:S(2)}) collective-permute-start(s16[2,1040,128]{2,1,0:T(8,128)(2,1)S(1)} %collective-permute-done.35.refs_2_), channel_id=1, source_target_pairs={{1,0},{2,1},{3,2},{5,4},{6,5},{7,6},{9,8},{10,9},{11,10},{13,12},{... | collective-permute-start | bytes 1597448 | tf_op jit(solution)/shard_map/ppermute | solution.py:571
  (38 other events, 484.9 us)

commit v2 on v1

--- a/solution.py
+++ b/solution.py
@@ -508,12 +508,20 @@
     return [(i, i ^ bit) for i in range(count)]
 
 
+def tree_sum(values):
+    while len(values) > 1:
+        values = [sum(values[i + 1 : i + 2], values[i]) for i in range(0, len(values), 2)]
+    return values[0]
+
+
 def shared_ratio(total, picture):
     count = lax.axis_size("wide")
     bit = 2
     while bit < count:
-        total = total + lax.ppermute(total, "wide", partner_of(count, bit))
-        bit *= 2
+        bits = [bit] if 2 * bit >= count else [bit, 2 * bit, 3 * bit]
+        arrived = [lax.ppermute(total, "wide", partner_of(count, b)) for b in bits]
+        total = tree_sum([total] + arrived)
+        bit *= 2 ** ((len(bits) + 1) // 2)
     return (picture - jnp.log(total + 1.0)).astype(jnp.bfloat16)
 
 

time: 199 us -> 186 us (0.935)
  waiting for transfers between devices: 68.5 us -> 56 us
    ppermute x16 -> x24, waiting for transfers between devices: 43 us -> 30.5 us  [shared_ratio(): arrived = [lax.ppermute(total, 'wide', partner_of(count, b)) for b in bits]]
    ppermute x16 -> x24, starting transfers between devices: 28.4 us -> 28.4 us  [shared_ratio(): arrived = [lax.ppermute(total, 'wide', partner_of(count, b)) for b in bits]]
  transfers between devices with their start and end apart: 41 -> 49, of which waited for: 29 -> 29; matrix products, arithmetic and copies ran while one was open for 4% -> 5% of each run, Pallas kernels for 9% -> 10%
where the time goes in v2:
time: 186 us; the launch traced here: 185 us
  waiting for transfers between devices  56 us (30%)
  Pallas kernels  55.4 us (30%)
  starting transfers between devices  54.2 us (29%)
  local copies, waits for them, and re-layouts  12.8 us (7%)
  other arithmetic  5.38 us (3%)
    ppermute x24, waiting for transfers between devices, shared_ratio(): arrived = [lax.ppermute(total, 'wide', partner_of(count, b)) for b in bits]  30.5 us
    ppermute x24, starting transfers between devices, shared_ratio(): arrived = [lax.ppermute(total, 'wide', partner_of(count, b)) for b in bits]  28.4 us
    pallas_call x1, Pallas kernels, window_correlations(): pl.pallas_call(functools.partial(window_body, count), out_shape=jax.Shape...  24 us
    pallas_call x23, Pallas kernels, sweep_step(): pl.pallas_call(functools.partial(sweep_body, back, forward), grid=(1,), i...  22.1 us
    ppermute x8, starting transfers between devices, shifted(): return lax.ppermute(value, axis, pairs)  17.8 us
    ppermute x8, waiting for transfers between devices, shifted(): return lax.ppermute(value, axis, pairs)  16.5 us
    ppermute x16, waiting for transfers between devices, swapped(): return lax.ppermute(value, 'wide', partner_of(count, 1))  8.97 us
    pallas_call x1, Pallas kernels, middle_spectra(): pl.pallas_call(functools.partial(middle_body, count), out_shape=[jax.Shap...  6.63 us
  transfers between devices with their start and end apart: 49, of which 29 were waited for; matrix products, arithmetic and copies ran while one was open for 5% of the time, Pallas kernels for 10%

profile of v2, /device:TPU:0, one launch (start us, length us, event | category | flops | bytes accessed | tf_op | source)
XLA Modules:
  0.0 185.0 jit_solution(9728370810294066274)
XLA Ops:
  2.3 5.2 %all-to-all-start = ((f32[8,4,18,128]{3,1,2,0:T(4,128)}), f32[8,4,18,128]{3,1,2,0:T(4,128)S(1)}, u32[]{:S(2)}, u32[]{:S(2)}) async-start(f32[8,4,18,128]{3,1,2,0:T(4,128)} %bitcast.4), calls=%async_computation | async-start | bytes 589824 | tf_op jit(solution)/shard_map/all_to_all | solution.py:547
  7.5 1.5 fusion.4
  10.1 1.6 copy.29
  16.4 1.9 %collective-permute-start.2 = (f32[144,128]{1,0:T(8,128)}, f32[144,128]{1,0:T(8,128)}, u32[]{:S(2)}, u32[]{:S(2)}) collective-permute-start(f32[144,128]{1,0:T(8,128)} %add.169), channel_id=1, source_target_pairs={{0,16},{4,20},{8,24},{12,28},{16,0},{20,4},{24,8},{28,12},{1,17},{... | collective-permute-start | bytes 221192 | tf_op jit(solution)/shard_map/ppermute | solution.py:522
  18.3 1.5 collective-permute-start.3
  22.1 2.5 %collective-permute-done.3 = f32[144,128]{1,0:T(8,128)} collective-permute-done((f32[144,128]{1,0:T(8,128)}, f32[144,128]{1,0:T(8,128)}, u32[]{:S(2)}, u32[]{:S(2)}) %collective-permute-start.3) | collective-permute-done | bytes 73760 | tf_op jit(solution)/shard_map/ppermute | solution.py:522
  31.8 1.5 collective-permute-start.7
  36.4 2.9 %collective-permute-done.8 = f32[144,128]{1,0:T(8,128)S(1)} collective-permute-done((f32[144,128]{1,0:T(8,128)S(1)}, f32[144,128]{1,0:T(8,128)S(1)}, u32[]{:S(2)}, u32[]{:S(2)}) %collective-permute-start.8) | collective-permute-done | bytes 73760 | tf_op jit(solution)/shard_map/ppermute | solution.py:522
  48.4 2.8 %collective-permute-done.13 = f32[144,128]{1,0:T(8,128)S(1)} collective-permute-done((f32[144,128]{1,0:T(8,128)S(1)}, f32[144,128]{1,0:T(8,128)S(1)}, u32[]{:S(2)}, u32[]{:S(2)}) %collective-permute-start.13) | collective-permute-done | bytes 73760 | tf_op jit(solution)/shard_map/ppermute | solution.py:522
  60.3 2.8 %collective-permute-done.18 = f32[144,128]{1,0:T(8,128)S(1)} collective-permute-done((f32[144,128]{1,0:T(8,128)S(1)}, f32[144,128]{1,0:T(8,128)S(1)}, u32[]{:S(2)}, u32[]{:S(2)}) %collective-permute-start.18) | collective-permute-done | bytes 73760 | tf_op jit(solution)/shard_map/ppermute | solution.py:522
  72.2 2.8 %collective-permute-done.23 = f32[144,128]{1,0:T(8,128)S(1)} collective-permute-done((f32[144,128]{1,0:T(8,128)S(1)}, f32[144,128]{1,0:T(8,128)S(1)}, u32[]{:S(2)}, u32[]{:S(2)}) %collective-permute-start.23) | collective-permute-done | bytes 73760 | tf_op jit(solution)/shard_map/ppermute | solution.py:522
  84.1 2.8 %collective-permute-done.28 = f32[144,128]{1,0:T(8,128)S(1)} collective-permute-done((f32[144,128]{1,0:T(8,128)S(1)}, f32[144,128]{1,0:T(8,128)S(1)}, u32[]{:S(2)}, u32[]{:S(2)}) %collective-permute-start.28) | collective-permute-done | bytes 73760 | tf_op jit(solution)/shard_map/ppermute | solution.py:522
  96.0 2.8 %collective-permute-done.33 = f32[144,128]{1,0:T(8,128)S(1)} collective-permute-done((f32[144,128]{1,0:T(8,128)S(1)}, f32[144,128]{1,0:T(8,128)S(1)}, u32[]{:S(2)}, u32[]{:S(2)}) %collective-permute-start.33) | collective-permute-done | bytes 73760 | tf_op jit(solution)/shard_map/ppermute | solution.py:522
  108.2 2.8 %collective-permute-done.38 = f32[144,128]{1,0:T(8,128)S(1)} collective-permute-done((f32[144,128]{1,0:T(8,128)S(1)}, f32[144,128]{1,0:T(8,128)S(1)}, u32[]{:S(2)}, u32[]{:S(2)}) %collective-permute-start.38) | collective-permute-done | bytes 73760 | tf_op jit(solution)/shard_map/ppermute | solution.py:522
  112.3 2.6 %last.1 = (f32[2,1024,128]{2,1,0:T(8,128)}, s16[2,1040,128]{2,1,0:T(8,128)(2,1)}) custom-call(s32[1]{0:T(128)} %bitcast.parity_ref, f32[1024,128]{1,0:T(8,128)S(1)} %sweep.43.volume_ref.refs_0_, f32[1024,128]{1,0:T(8,128)S(1)} %get-tuple-element.32.refs_1_, bf16[144,128]{1,0:T(8,128)(2,1)S(1)} %subtract_convert_fusion.refs_2_, ...), custom_call_target="tpu_custom_call" | custom-call | tf_op jit(solution)/shard_map/last/pallas_call | solution.py:487
  114.9 4.3 %collective-permute-start.40 = (s16[2,1040,128]{2,1,0:T(8,128)(2,1)}, s16[2,1040,128]{2,1,0:T(8,128)(2,1)}, u32[]{:S(2)}, u32[]{:S(2)}) collective-permute-start(s16[2,1040,128]{2,1,0:T(8,128)(2,1)} %get-tuple-element.35), channel_id=1, source_target_pairs={{0,1},{1,2},{2,3},{4,5},{5,6},{6,7},{8,9},{9,10},{10,11},{12,13},{... | collective-permute-start | bytes 1597448 | tf_op jit(solution)/shard_map/ppermute | solution.py:579
  121.8 3.1 %collective-permute-start.42 = (s16[2,1040,128]{2,1,0:T(8,128)(2,1)}, s16[2,1040,128]{2,1,0:T(8,128)(2,1)S(1)}, u32[]{:S(2)}, u32[]{:S(2)}) collective-permute-start(s16[2,1040,128]{2,1,0:T(8,128)(2,1)} %get-tuple-element.35), channel_id=1, source_target_pairs={{0,4},{4,8},{8,12},{12,16},{16,20},{20,24},{24,28},{1,5},{5,9},{9,... | collective-permute-start | bytes 1597448 | tf_op jit(solution)/shard_map/ppermute | solution.py:579
  124.9 5.5 %collective-permute-done.40.near = s16[2,1040,128]{2,1,0:T(8,128)(2,1)} collective-permute-done((s16[2,1040,128]{2,1,0:T(8,128)(2,1)}, s16[2,1040,128]{2,1,0:T(8,128)(2,1)}, u32[]{:S(2)}, u32[]{:S(2)}) %collective-permute-start.40) | collective-permute-done | bytes 532512 | tf_op jit(solution)/shard_map/ppermute | solution.py:579
  131.7 3.6 %collective-permute-done.41.far = s16[2,1040,128]{2,1,0:T(8,128)(2,1)} collective-permute-done((s16[2,1040,128]{2,1,0:T(8,128)(2,1)}, s16[2,1040,128]{2,1,0:T(8,128)(2,1)}, u32[]{:S(2)}, u32[]{:S(2)}) %collective-permute-start.41) | collective-permute-done | bytes 532512 | tf_op jit(solution)/shard_map/ppermute | solution.py:579
  136.6 4.0 %collective-permute-start.46 = (s16[2,1040,128]{2,1,0:T(8,128)(2,1)S(1)}, s16[2,1040,128]{2,1,0:T(8,128)(2,1)}, u32[]{:S(2)}, u32[]{:S(2)}) collective-permute-start(s16[2,1040,128]{2,1,0:T(8,128)(2,1)S(1)} %collective-permute-done.43.refs_2_), channel_id=1, source_target_pairs={{0,1},{1,2},{2,3},{4,5},{5,6},{6,7},{8,9},{9,10},{10,11},{12,13},{... | collective-permute-start | bytes 1597448 | tf_op jit(solution)/shard_map/ppermute | solution.py:579
  143.5 6.6 %middle.1 = (f32[4,72,32,128]{3,2,1,0:T(8,128)S(1)}, f32[4,8,128]{2,1,0:T(8,128)S(1)}) custom-call(s32[4,3]{1,0:T(4,128)S(1)} %pad_add_fusion.starts, f32[2,1024,128]{2,1,0:T(8,128)S(1)} %copy-done.5, s16[2,1040,128]{2,1,0:T(8,128)(2,1)} %collective-permute-done.40.near, s16[2,1040,128]{2,1,0:T(8,128)(2,1)} %collective-permute-done.41.far, ...), custom_call_target="tpu_custom_call" | custom-call | tf_op jit(solution)/shard_map/middle/pallas_call | solution.py:313
  150.2 1.8 collective-permute-done.46.refs_5_
  152.0 5.6 %collective-permute-done.47.refs_6_ = s16[2,1040,128]{2,1,0:T(8,128)(2,1)} collective-permute-done((s16[2,1040,128]{2,1,0:T(8,128)(2,1)S(1)}, s16[2,1040,128]{2,1,0:T(8,128)(2,1)}, u32[]{:S(2)}, u32[]{:S(2)}) %collective-permute-start.47) | collective-permute-done | bytes 532512 | tf_op jit(solution)/shard_map/ppermute | solution.py:579
  159.5 24.0 %windows.1 = f32[16,2048]{1,0:T(8,128)S(1)} custom-call(s32[4,3]{1,0:T(4,128)S(1)} %pad_add_fusion.starts, f32[4,8,128]{2,1,0:T(8,128)S(1)} %get-tuple-element.36.stats, f32[4,72,32,128]{3,2,1,0:T(8,128)S(1)} %get-tuple-element.37.refs_0_, s16[2,1040,128]{2,1,0:T(8,128)(2,1)S(1)} %collective-permute-done.42.refs_1_, ...), custom_call_target="tpu_custom_call" | custom-call | tf_op jit(solution)/shard_map/windows/pallas_call | solution.py:341
  (178 shorter events, 87.4 us)
Async XLA Ops:
  2.3 17.6 %all-to-all-start = ((f32[8,4,18,128]{3,1,2,0:T(4,128)}), f32[8,4,18,128]{3,1,2,0:T(4,128)S(1)}, u32[]{:S(2)}, u32[]{:S(2)}) async-start(f32[8,4,18,128]{3,1,2,0:T(4,128)} %bitcast.4), calls=%async_computation | async-start | bytes 589824 | tf_op jit(solution)/shard_map/all_to_all | solution.py:547
  16.4 5.7 %collective-permute-start.2 = (f32[144,128]{1,0:T(8,128)}, f32[144,128]{1,0:T(8,128)}, u32[]{:S(2)}, u32[]{:S(2)}) collective-permute-start(f32[144,128]{1,0:T(8,128)} %add.169), channel_id=1, source_target_pairs={{0,16},{4,20},{8,24},{12,28},{16,0},{20,4},{24,8},{28,12},{1,17},{... | collective-permute-start | bytes 221192 | tf_op jit(solution)/shard_map/ppermute | solution.py:522
  18.3 6.3 %collective-permute-start.3 = (f32[144,128]{1,0:T(8,128)}, f32[144,128]{1,0:T(8,128)}, u32[]{:S(2)}, u32[]{:S(2)}) collective-permute-start(f32[144,128]{1,0:T(8,128)} %add.169), channel_id=1, source_target_pairs={{0,24},{4,28},{8,16},{12,20},{16,8},{20,12},{24,0},{28,4},{1,25},{... | collective-permute-start | bytes 221192 | tf_op jit(solution)/shard_map/ppermute | solution.py:522
  19.8 4.8 %collective-permute-start.1 = (f32[144,128]{1,0:T(8,128)}, f32[144,128]{1,0:T(8,128)}, u32[]{:S(2)}, u32[]{:S(2)}) collective-permute-start(f32[144,128]{1,0:T(8,128)} %add.169), channel_id=1, source_target_pairs={{0,8},{4,12},{8,0},{12,4},{16,24},{20,28},{24,16},{28,20},{1,9},{5... | collective-permute-start | bytes 221192 | tf_op jit(solution)/shard_map/ppermute | solution.py:522
  33.3 6.0 %collective-permute-start.8 = (f32[144,128]{1,0:T(8,128)S(1)}, f32[144,128]{1,0:T(8,128)S(1)}, u32[]{:S(2)}, u32[]{:S(2)}) collective-permute-start(f32[144,128]{1,0:T(8,128)S(1)} %add.174), channel_id=1, source_target_pairs={{0,24},{4,28},{8,16},{12,20},{16,8},{20,12},{24,0},{28,4},{1,25},{... | collective-permute-start | bytes 221192 | tf_op jit(solution)/shard_map/ppermute | solution.py:522
  45.3 5.9 %collective-permute-start.13 = (f32[144,128]{1,0:T(8,128)S(1)}, f32[144,128]{1,0:T(8,128)S(1)}, u32[]{:S(2)}, u32[]{:S(2)}) collective-permute-start(f32[144,128]{1,0:T(8,128)S(1)} %add.179), channel_id=1, source_target_pairs={{0,24},{4,28},{8,16},{12,20},{16,8},{20,12},{24,0},{28,4},{1,25},{... | collective-permute-start | bytes 221192 | tf_op jit(solution)/shard_map/ppermute | solution.py:522
  57.2 5.9 %collective-permute-start.18 = (f32[144,128]{1,0:T(8,128)S(1)}, f32[144,128]{1,0:T(8,128)S(1)}, u32[]{:S(2)}, u32[]{:S(2)}) collective-permute-start(f32[144,128]{1,0:T(8,128)S(1)} %add.184), channel_id=1, source_target_pairs={{0,24},{4,28},{8,16},{12,20},{16,8},{20,12},{24,0},{28,4},{1,25},{... | collective-permute-start | bytes 221192 | tf_op jit(solution)/shard_map/ppermute | solution.py:522
  58.3 4.8 %collective-permute-start.16 = (f32[144,128]{1,0:T(8,128)S(1)}, f32[144,128]{1,0:T(8,128)S(1)}, u32[]{:S(2)}, u32[]{:S(2)}) collective-permute-start(f32[144,128]{1,0:T(8,128)S(1)} %add.184), channel_id=1, source_target_pairs={{0,8},{4,12},{8,0},{12,4},{16,24},{20,28},{24,16},{28,20},{1,9},{5... | collective-permute-start | bytes 221192 | tf_op jit(solution)/shard_map/ppermute | solution.py:522
  69.1 5.9 %collective-permute-start.23 = (f32[144,128]{1,0:T(8,128)S(1)}, f32[144,128]{1,0:T(8,128)S(1)}, u32[]{:S(2)}, u32[]{:S(2)}) collective-permute-start(f32[144,128]{1,0:T(8,128)S(1)} %add.189), channel_id=1, source_target_pairs={{0,24},{4,28},{8,16},{12,20},{16,8},{20,12},{24,0},{28,4},{1,25},{... | collective-permute-start | bytes 221192 | tf_op jit(solution)/shard_map/ppermute | solution.py:522
  70.2 4.8 %collective-permute-start.21 = (f32[144,128]{1,0:T(8,128)S(1)}, f32[144,128]{1,0:T(8,128)S(1)}, u32[]{:S(2)}, u32[]{:S(2)}) collective-permute-start(f32[144,128]{1,0:T(8,128)S(1)} %add.189), channel_id=1, source_target_pairs={{0,8},{4,12},{8,0},{12,4},{16,24},{20,28},{24,16},{28,20},{1,9},{5... | collective-permute-start | bytes 221192 | tf_op jit(solution)/shard_map/ppermute | solution.py:522
  80.9 5.9 %collective-permute-start.28 = (f32[144,128]{1,0:T(8,128)S(1)}, f32[144,128]{1,0:T(8,128)S(1)}, u32[]{:S(2)}, u32[]{:S(2)}) collective-permute-start(f32[144,128]{1,0:T(8,128)S(1)} %add.194), channel_id=1, source_target_pairs={{0,24},{4,28},{8,16},{12,20},{16,8},{20,12},{24,0},{28,4},{1,25},{... | collective-permute-start | bytes 221192 | tf_op jit(solution)/shard_map/ppermute | solution.py:522
  82.1 4.8 %collective-permute-start.26 = (f32[144,128]{1,0:T(8,128)S(1)}, f32[144,128]{1,0:T(8,128)S(1)}, u32[]{:S(2)}, u32[]{:S(2)}) collective-permute-start(f32[144,128]{1,0:T(8,128)S(1)} %add.194), channel_id=1, source_target_pairs={{0,8},{4,12},{8,0},{12,4},{16,24},{20,28},{24,16},{28,20},{1,9},{5... | collective-permute-start | bytes 221192 | tf_op jit(solution)/shard_map/ppermute | solution.py:522
  92.8 5.9 %collective-permute-start.33 = (f32[144,128]{1,0:T(8,128)S(1)}, f32[144,128]{1,0:T(8,128)S(1)}, u32[]{:S(2)}, u32[]{:S(2)}) collective-permute-start(f32[144,128]{1,0:T(8,128)S(1)} %add.199), channel_id=1, source_target_pairs={{0,24},{4,28},{8,16},{12,20},{16,8},{20,12},{24,0},{28,4},{1,25},{... | collective-permute-start | bytes 221192 | tf_op jit(solution)/shard_map/ppermute | solution.py:522
  94.0 4.8 %collective-permute-start.31 = (f32[144,128]{1,0:T(8,128)S(1)}, f32[144,128]{1,0:T(8,128)S(1)}, u32[]{:S(2)}, u32[]{:S(2)}) collective-permute-start(f32[144,128]{1,0:T(8,128)S(1)} %add.199), channel_id=1, source_target_pairs={{0,8},{4,12},{8,0},{12,4},{16,24},{20,28},{24,16},{28,20},{1,9},{5... | collective-permute-start | bytes 221192 | tf_op jit(solution)/shard_map/ppermute | solution.py:522
  105.0 5.9 %collective-permute-start.38 = (f32[144,128]{1,0:T(8,128)S(1)}, f32[144,128]{1,0:T(8,128)S(1)}, u32[]{:S(2)}, u32[]{:S(2)}) collective-permute-start(f32[144,128]{1,0:T(8,128)S(1)} %add.204), channel_id=1, source_target_pairs={{0,24},{4,28},{8,16},{12,20},{16,8},{20,12},{24,0},{28,4},{1,25},{... | collective-permute-start | bytes 221192 | tf_op jit(solution)/shard_map/ppermute | solution.py:522
  106.2 4.8 %collective-permute-start.36 = (f32[144,128]{1,0:T(8,128)S(1)}, f32[144,128]{1,0:T(8,128)S(1)}, u32[]{:S(2)}, u32[]{:S(2)}) collective-permute-start(f32[144,128]{1,0:T(8,128)S(1)} %add.204), channel_id=1, source_target_pairs={{0,8},{4,12},{8,0},{12,4},{16,24},{20,28},{24,16},{28,20},{1,9},{5... | collective-permute-start | bytes 221192 | tf_op jit(solution)/shard_map/ppermute | solution.py:522
  114.9 15.5 %collective-permute-start.40 = (s16[2,1040,128]{2,1,0:T(8,128)(2,1)}, s16[2,1040,128]{2,1,0:T(8,128)(2,1)}, u32[]{:S(2)}, u32[]{:S(2)}) collective-permute-start(s16[2,1040,128]{2,1,0:T(8,128)(2,1)} %get-tuple-element.35), channel_id=1, source_target_pairs={{0,1},{1,2},{2,3},{4,5},{5,6},{6,7},{8,9},{9,10},{10,11},{12,13},{... | collective-permute-start | bytes 1597448 | tf_op jit(solution)/shard_map/ppermute | solution.py:579
  119.2 16.1 %collective-permute-start.41 = (s16[2,1040,128]{2,1,0:T(8,128)(2,1)}, s16[2,1040,128]{2,1,0:T(8,128)(2,1)}, u32[]{:S(2)}, u32[]{:S(2)}) collective-permute-start(s16[2,1040,128]{2,1,0:T(8,128)(2,1)} %get-tuple-element.35), channel_id=1, source_target_pairs={{1,0},{2,1},{3,2},{5,4},{6,5},{7,6},{9,8},{10,9},{11,10},{13,12},{... | collective-permute-start | bytes 1597448 | tf_op jit(solution)/shard_map/ppermute | solution.py:579
  120.5 16.1 %collective-permute-start.43 = (s16[2,1040,128]{2,1,0:T(8,128)(2,1)}, s16[2,1040,128]{2,1,0:T(8,128)(2,1)S(1)}, u32[]{:S(2)}, u32[]{:S(2)}) collective-permute-start(s16[2,1040,128]{2,1,0:T(8,128)(2,1)} %get-tuple-element.35), channel_id=1, source_target_pairs={{4,0},{8,4},{12,8},{16,12},{20,16},{24,20},{28,24},{5,1},{9,5},{13... | collective-permute-start | bytes 1597448 | tf_op jit(solution)/shard_map/ppermute | solution.py:579
  121.8 28.3 %collective-permute-start.42 = (s16[2,1040,128]{2,1,0:T(8,128)(2,1)}, s16[2,1040,128]{2,1,0:T(8,128)(2,1)S(1)}, u32[]{:S(2)}, u32[]{:S(2)}) collective-permute-start(s16[2,1040,128]{2,1,0:T(8,128)(2,1)} %get-tuple-element.35), channel_id=1, source_target_pairs={{0,4},{4,8},{8,12},{12,16},{16,20},{20,24},{24,28},{1,5},{5,9},{9,... | collective-permute-start | bytes 1597448 | tf_op jit(solution)/shard_map/ppermute | solution.py:579
  130.4 19.8 %collective-permute-start.44 = (s16[2,1040,128]{2,1,0:T(8,128)(2,1)}, s16[2,1040,128]{2,1,0:T(8,128)(2,1)S(1)}, u32[]{:S(2)}, u32[]{:S(2)}) collective-permute-start(s16[2,1040,128]{2,1,0:T(8,128)(2,1)} %collective-permute-done.40.near), channel_id=1, source_target_pairs={{0,4},{4,8},{8,12},{12,16},{16,20},{20,24},{24,28},{1,5},{5,9},{9,... | collective-permute-start | bytes 1597448 | tf_op jit(solution)/shard_map/ppermute | solution.py:579
  135.3 14.9 %collective-permute-start.45 = (s16[2,1040,128]{2,1,0:T(8,128)(2,1)}, s16[2,1040,128]{2,1,0:T(8,128)(2,1)S(1)}, u32[]{:S(2)}, u32[]{:S(2)}) collective-permute-start(s16[2,1040,128]{2,1,0:T(8,128)(2,1)} %collective-permute-done.41.far), channel_id=1, source_target_pairs={{0,4},{4,8},{8,12},{12,16},{16,20},{20,24},{24,28},{1,5},{5,9},{9,... | collective-permute-start | bytes 1597448 | tf_op jit(solution)/shard_map/ppermute | solution.py:579
  136.6 15.4 %collective-permute-start.46 = (s16[2,1040,128]{2,1,0:T(8,128)(2,1)S(1)}, s16[2,1040,128]{2,1,0:T(8,128)(2,1)}, u32[]{:S(2)}, u32[]{:S(2)}) collective-permute-start(s16[2,1040,128]{2,1,0:T(8,128)(2,1)S(1)} %collective-permute-done.43.refs_2_), channel_id=1, source_target_pairs={{0,1},{1,2},{2,3},{4,5},{5,6},{6,7},{8,9},{9,10},{10,11},{12,13},{... | collective-permute-start | bytes 1597448 | tf_op jit(solution)/shard_map/ppermute | solution.py:579
  140.6 17.0 %collective-permute-start.47 = (s16[2,1040,128]{2,1,0:T(8,128)(2,1)S(1)}, s16[2,1040,128]{2,1,0:T(8,128)(2,1)}, u32[]{:S(2)}, u32[]{:S(2)}) collective-permute-start(s16[2,1040,128]{2,1,0:T(8,128)(2,1)S(1)} %collective-permute-done.43.refs_2_), channel_id=1, source_target_pairs={{1,0},{2,1},{3,2},{5,4},{6,5},{7,6},{9,8},{10,9},{11,10},{13,12},{... | collective-permute-start | bytes 1597448 | tf_op jit(solution)/shard_map/ppermute | solution.py:579
  (46 other events, 497.3 us)
